TPU v7x, 256 devices: a whole 4x4x8 slice. The times are simulated.
256 devices in a mesh: lat: 64 (over z_lo, y, x), depth: 4 (over z_hi, core).
Axes of the slice: x: 4, y: 4, z: 8 (z_hi: 2, z_lo: 4; z = z_hi * 4 + z_lo), core: 2. Of those that a mesh axis runs over, the one named last changes fastest.
Arguments:
- velocity_fine: float32 [3, 768, 64, 384], P(None, 'lat', 'depth'), may hold values from -6 to 6
- stress_fine: float32 [6, 768, 64, 384], P(None, 'lat', 'depth'), may hold values from -6 to 6
- memory_fine: float32 [6, 768, 64, 384], P(None, 'lat', 'depth'), may hold values from -1.8 to 1.8
- peak_fine: float32 [768, 64, 384], P('lat', 'depth'), may hold values from 0 to 12
- zone_fine: int32 [768, 64, 384], P('lat', 'depth'), may hold values from 0 to 7
- velocity_coarse: float32 [3, 256, 128, 128], P(None, 'lat', 'depth'), may hold values from -6 to 6
- stress_coarse: float32 [6, 256, 128, 128], P(None, 'lat', 'depth'), may hold values from -6 to 6
- memory_coarse: float32 [6, 256, 128, 128], P(None, 'lat', 'depth'), may hold values from -1.8 to 1.8
- peak_coarse: float32 [256, 128, 128], P('lat', 'depth'), may hold values from 0 to 12
- zone_coarse: int32 [256, 128, 128], P('lat', 'depth'), may hold values from 0 to 7
- zone_table: float32 [8, 5], replicated, may hold values from 0.05 to 1, as said below
- interp_weight: int32 [2, 3], replicated, may hold values from 0 to 8
- restrict_weight: int32 [2, 3], replicated, may hold values from 1 to 8
Outputs:
- fine_velocity: float32 [3, 768, 64, 384], P(None, 'lat', 'depth')
- fine_stress: float32 [6, 768, 64, 384], P(None, 'lat', 'depth')
- fine_memory: float32 [6, 768, 64, 384], P(None, 'lat', 'depth')
- fine_peak: float32 [768, 64, 384], P('lat', 'depth')
- coarse_velocity: float32 [3, 256, 128, 128], P(None, 'lat', 'depth')
- coarse_stress: float32 [6, 256, 128, 128], P(None, 'lat', 'depth')
- coarse_memory: float32 [6, 256, 128, 128], P(None, 'lat', 'depth')
- coarse_peak: float32 [256, 128, 128], P('lat', 'depth')
Inputs may be any that keep to these rules, and one draw needn't show every extreme that they name: `zone_table`: column 0 lies in 0.5 to 1, columns 1 and 2 in 0.1 to 0.3, column 3 in 0.5 to 0.95, column 4 in 0.05 to 0.3.
All inputs are finite; a program needn't handle non-finite values.
Results may differ from a plain program's by a relative error of at most 0.0003.
Values sent between devices are 32-bit elements; how exact they have to be, the bound alone decides.
No kernel may reach another device: no remote copies, remote signals or barrier semaphores. Data moves between devices by JAX's collectives and lax.ppermute only.
A program may use at most 128 MiB of HBM per device.

v0:
```python
import functools

import jax
import jax.numpy as jnp
from jax import lax
from jax.experimental import pallas as pl
from jax.experimental.pallas import tpu as pltpu
from jax.sharding import PartitionSpec as P

STEPS = 2
DT = 0.4
NEAR = 9.0 / 8.0
FAR = 1.0 / 24.0
TINY = 1e-36

STRESS_X = ([(0, 1), (3, 2), (3, 1), (4, 2), (4, 1)], [(0, 0), (0, 1), (3, 0), (4, 0)])
STRESS_Z = ([(4, 2), (4, 1), (5, 2), (5, 1), (2, 1)], [(4, 0), (5, 0), (2, 0), (2, 1)])
VELOCITY_X = ([(0, 2), (0, 1), (1, 1), (2, 1)], [(0, 0), (1, 0), (1, 1), (2, 0), (2, 1)])
VELOCITY_Z = ([(2, 2), (2, 1), (0, 1), (1, 1)], [(2, 0), (0, 0), (0, 1), (1, 0), (1, 1)])

CB, LAME, MU2, DECAY, DAMP, ISO, SCALE = range(7)


class Sizes:
    def __init__(self, fine, coarse):
        self.fx, self.fz, self.fy = fine
        self.cx, self.cz, self.cy = coarse
        self.lanes = self.fy // self.cy
        self.lat_fine = 5 * self.fz
        self.lat_rows = self.lat_fine + -(-5 // self.lanes) * self.cz
        self.dep_fine = 5 * self.fx
        used = self.dep_fine + 5 * -(-self.cx // self.lanes)
        self.dep_rows = -(-used // 8) * 8

    def lat_slot(self, k):
        row = self.lat_fine + (k // self.lanes) * self.cz
        lane = (k % self.lanes) * self.cy
        return (slice(row, row + self.cz), slice(lane, lane + self.cy))

    def dep_slot(self, k, x):
        row = self.dep_fine + (x // self.lanes) * 5 + k
        lane = (x % self.lanes) * self.cy
        return (slice(row, row + 1), slice(lane, lane + self.cy))


def y_shift(f, offset, lane):
    width = f.shape[1]
    moved = pltpu.roll(f, (-offset) % width, 1)
    inside = lane < width - offset if offset > 0 else lane >= -offset
    return jnp.where(inside, moved, 0.0)


def z_shift(f, offset, row, low, high):
    depth = f.shape[0]
    moved = pltpu.roll(f, (-offset) % depth, 0)
    if offset < 0:
        for j in range(-offset):
            moved = jnp.where(row == j, low[offset + j], moved)
    else:
        for j in range(offset):
            moved = jnp.where(row == depth - offset + j, high[j], moved)
    return moved


def y_parts(f, up, lane):
    if up:
        return y_shift(f, 1, lane) - f, y_shift(f, 2, lane) - y_shift(f, -1, lane)
    return f - y_shift(f, -1, lane), y_shift(f, 1, lane) - y_shift(f, -2, lane)


def z_parts(f, up, row, low, high):
    def at(offset):
        return z_shift(f, offset, row, low, high)

    if up:
        return at(1) - f, at(2) - at(-1)
    return f - at(-1), at(1) - at(-2)


def x_parts(get, x, up):
    if up:
        return get(x + 1) - get(x), get(x + 2) - get(x - 1)
    return get(x) - get(x - 1), get(x + 1) - get(x - 2)


class Grid:
    def __init__(self, sizes, fine, field, x_lists, z_lists, xlo, xhi, zlo, zhi):
        self.sizes, self.fine, self.field = sizes, fine, field
        self.x_lists, self.z_lists = x_lists, z_lists
        self.xlo, self.xhi, self.zlo, self.zhi = xlo, xhi, zlo, zhi
        self.nx = sizes.fx if fine else sizes.cx
        self.nz = sizes.fz if fine else sizes.cz
        self.ny = sizes.fy if fine else sizes.cy
        self.row = lax.broadcasted_iota(jnp.int32, (self.nz, self.ny), 0)
        self.lane = lax.broadcasted_iota(jnp.int32, (self.nz, self.ny), 1)

    def x_layer(self, ref, k):
        if self.fine:
            return ref[k * self.nz : (k + 1) * self.nz, :]
        return ref[self.sizes.lat_slot(k)]

    def x_get(self, comp):
        def get(x):
            if isinstance(x, int) and x < 0:
                return self.x_layer(self.xlo, self.x_lists[0].index((comp, -x)))
            if isinstance(x, int) and x >= self.nx:
                return self.x_layer(self.xhi, self.x_lists[1].index((comp, x - self.nx)))
            return self.field[comp, x]

        return get

    def z_row(self, ref, k, x):
        if not self.fine:
            return ref[self.sizes.dep_slot(k, x)]
        if isinstance(x, int):
            return ref[k * self.nx + x : k * self.nx + x + 1, :]
        return ref[pl.ds(k * self.nx + x, 1), :]

    def z_halo(self, comp, x):
        low = {-r: self.z_row(self.zlo, k, x) for k, (c, r) in enumerate(self.z_lists[0]) if c == comp}
        high = {r: self.z_row(self.zhi, k, x) for k, (c, r) in enumerate(self.z_lists[1]) if c == comp}
        return low, high

    def dx(self, comp, x, up):
        return x_parts(self.x_get(comp), x, up)

    def dy(self, comp, x, up):
        return y_parts(self.field[comp, x], up, self.lane)

    def dz(self, comp, x, up):
        low, high = self.z_halo(comp, x)
        return z_parts(self.field[comp, x], up, self.row, low, high)

    def rows(self, body):
        if self.nx > 8:

            def step(x, carry):
                body(x)
                return carry

            for x in (0, 1):
                body(x)
            lax.fori_loop(2, self.nx - 2, step, 0)
            for x in (self.nx - 2, self.nx - 1):
                body(x)
        else:
            for x in range(self.nx):
                body(x)


def combine(*parts):
    near = functools.reduce(lambda a, b: a + b, [p[0] for p in parts])
    far = functools.reduce(lambda a, b: a + b, [p[1] for p in parts])
    return NEAR * near - FAR * far


def velocity_rows(grid, velocity, out, props):
    scale = DT if grid.fine else DT / 3.0

    def body(x):
        speed = scale * props[CB, x]
        ax = combine(grid.dx(0, x, True), grid.dy(3, x, False), grid.dz(4, x, False))
        out[0, x] = velocity[0, x] + speed * ax
        ay = combine(grid.dx(3, x, False), grid.dy(1, x, True), grid.dz(5, x, False))
        out[1, x] = velocity[1, x] + speed * ay
        az = combine(grid.dx(4, x, False), grid.dy(5, x, False), grid.dz(2, x, True))
        out[2, x] = velocity[2, x] + speed * az

    grid.rows(body)


def stress_rows(grid, stress, memory, stress_out, memory_out, props):
    inverse = 1.0 if grid.fine else 1.0 / 3.0

    def body(x):
        lame, twice = props[LAME, x], props[MU2, x]
        decay, damp = props[DECAY, x], props[DAMP, x]
        if inverse != 1.0:
            lame, twice = lame * inverse, twice * inverse
        half = 0.5 * twice

        def finish(comp, rate):
            old = memory[comp, x]
            new = decay * old - damp * rate
            memory_out[comp, x] = new
            stress_out[comp, x] = stress[comp, x] + DT * (rate + 0.5 * (old + new))

        xx = combine(grid.dx(0, x, False))
        yy = combine(grid.dy(1, x, False))
        zz = combine(grid.dz(2, x, False))
        volume = lame * (xx + yy + zz)
        finish(0, volume + twice * xx)
        finish(1, volume + twice * yy)
        finish(2, volume + twice * zz)
        finish(3, half * combine(grid.dy(0, x, True), grid.dx(1, x, True)))
        finish(4, half * combine(grid.dz(0, x, True), grid.dx(2, x, True)))
        finish(5, half * combine(grid.dz(1, x, True), grid.dy(2, x, True)))

    grid.rows(body)


def receive(sizes, place, latE, latO, depE, depO, diag, z_lists, weights, xlo, xhi, zlo, zhi, lift):
    lat, depth = place[0], place[1]
    lat_even, depth_even = lax.rem(lat, 2) == 0, lax.rem(depth, 2) == 0
    last_lat, last_depth = place[2] - 1, place[3] - 1

    @pl.when(lat_even)
    def _():
        xlo[...] = latO[...]
        xhi[...] = latE[...]

    @pl.when(jnp.logical_not(lat_even))
    def _():
        xlo[...] = latE[...]
        xhi[...] = latO[...]

    @pl.when(lat == 0)
    def _():
        xlo[...] = jnp.zeros_like(xlo)

    @pl.when(lat == last_lat)
    def _():
        xhi[...] = jnp.zeros_like(xhi)

    @pl.when(depth_even)
    def _():
        zlo[...] = depO[...]
        zhi[...] = depE[...]

    @pl.when(jnp.logical_not(depth_even))
    def _():
        zlo[...] = depE[...]
        zhi[...] = depO[...]

    @pl.when(depth == 0)
    def _():
        zlo[0 : sizes.dep_fine, :] = jnp.zeros((sizes.dep_fine, sizes.fy), jnp.float32)

    @pl.when(depth == last_depth)
    def _():
        interp = weights
        count = len(z_lists[1])
        lift[...] = jnp.zeros_like(lift)
        beyond = jnp.where(lat == last_lat, 0.0, 1.0)
        for k in range(count):
            planes = [depO[sizes.dep_slot(k, a)] for a in range(sizes.cx)]
            planes.append(diag[k : k + 1, :] * beyond)
            for a in range(sizes.cx):
                for p in range(3):
                    share = interp[0, p].astype(jnp.float32) * 0.125
                    x = k * sizes.fx + 3 * a + p
                    lift[x : x + 1, :] = share * planes[a] + (1.0 - share) * planes[a + 1]
        c = lax.broadcasted_iota(jnp.int32, (sizes.cy, sizes.fy), 0)
        f = lax.broadcasted_iota(jnp.int32, (sizes.cy, sizes.fy), 1)
        gap = f - 3 * c
        spread = jnp.zeros((sizes.cy, sizes.fy), jnp.float32)
        for p in range(3):
            share = interp[1, p].astype(jnp.float32) * 0.125
            spread = jnp.where(gap == p, share, spread)
            spread = jnp.where(gap == p - 3, 1.0 - share, spread)
        ghost = jnp.dot(
            lift[...], spread, precision=lax.Precision.HIGHEST, preferred_element_type=jnp.float32
        )
        zhi[...] = jnp.zeros_like(zhi)
        zhi[0 : sizes.dep_fine, :] = ghost[0 : sizes.dep_fine, :]


def send(sizes, place, fine, coarse, x_lists, z_lists, weights, latE, latO, depE, depO, diag, gather):
    lat, depth = place[0], place[1]
    lat_even, depth_even = lax.rem(lat, 2) == 0, lax.rem(depth, 2) == 0
    last_depth = place[3] - 1

    def pack_x(up, down):
        for ref, entries, high in ((up, x_lists[0], True), (down, x_lists[1], False)):
            for k, (comp, r) in enumerate(entries):
                ref[k * sizes.fz : (k + 1) * sizes.fz, :] = fine[comp, sizes.fx - r if high else r]
                ref[sizes.lat_slot(k)] = coarse[comp, sizes.cx - r if high else r]

    def pack_z(up, down):
        for ref, entries, high in ((up, z_lists[0], True), (down, z_lists[1], False)):
            for k, (comp, r) in enumerate(entries):
                z = sizes.fz - r if high else r
                for x in range(sizes.fx):
                    ref[k * sizes.fx + x : k * sizes.fx + x + 1, :] = fine[comp, x, z : z + 1, :]
                z = sizes.cz - r if high else r
                for x in range(sizes.cx):
                    ref[sizes.dep_slot(k, x)] = coarse[comp, x, z : z + 1, :]

    @pl.when(lat_even)
    def _():
        pack_x(latE, latO)

    @pl.when(jnp.logical_not(lat_even))
    def _():
        pack_x(latO, latE)

    @pl.when(depth_even)
    def _():
        pack_z(depE, depO)

    @pl.when(jnp.logical_not(depth_even))
    def _():
        pack_z(depO, depE)

    diag[...] = jnp.zeros_like(diag)

    @pl.when(depth == 0)
    def _():
        for k, (comp, j) in enumerate(z_lists[1]):
            for x in range(sizes.cx):
                plane = ((2.0 - j) * coarse[comp, x, 0:1, :] + (1.0 + j) * coarse[comp, x, 1:2, :]) / 3.0
                depO[sizes.dep_slot(k, x)] = plane
                if x == 0:
                    diag[k : k + 1, :] = plane

    @pl.when(depth == last_depth)
    def _():
        restrict = weights
        wx = [restrict[0, p].astype(jnp.float32) for p in range(3)]
        wy = [restrict[1, p].astype(jnp.float32) for p in range(3)]
        gather[...] = jnp.zeros_like(gather)
        for k, (comp, r) in enumerate(z_lists[0]):
            z = sizes.fz - 3 * r
            for a in range(sizes.cx):
                total = None
                for p in range(3):
                    f = fine[comp, 3 * a + p, z : z + 3, :]
                    layers = wx[p] * (f[0:1] + f[1:2] + f[2:3])
                    total = layers if total is None else total + layers
                row = k * sizes.cx + a
                gather[row : row + 1, :] = total
        f = lax.broadcasted_iota(jnp.int32, (sizes.fy, sizes.cy), 0)
        c = lax.broadcasted_iota(jnp.int32, (sizes.fy, sizes.cy), 1)
        gap = f - 3 * c
        table = jnp.zeros((sizes.fy, sizes.cy), jnp.float32)
        for p in range(3):
            table = jnp.where(gap == p, wy[p], table)
        summed = jnp.dot(
            gather[...], table, precision=lax.Precision.HIGHEST, preferred_element_type=jnp.float32
        )
        norm = jnp.full((1, sizes.cy), 3.0 * (wx[0] + wx[1] + wx[2]) * (wy[0] + wy[1] + wy[2]))
        lifted = summed / norm
        for k in range(len(z_lists[0])):
            for a in range(sizes.cx):
                row = k * sizes.cx + a
                depO[sizes.dep_slot(k, a)] = lifted[row : row + 1, :]


SMEM = pl.BlockSpec(memory_space=pltpu.SMEM)
VMEM = pl.BlockSpec(memory_space=pltpu.VMEM)
LIMIT = 48 * 1024 * 1024


def packs(sizes):
    lat = jax.ShapeDtypeStruct((sizes.lat_rows, sizes.fy), jnp.float32)
    dep = jax.ShapeDtypeStruct((sizes.dep_rows, sizes.fy), jnp.float32)
    return [lat, lat, dep, dep, jax.ShapeDtypeStruct((8, sizes.cy), jnp.float32)]


def halo_scratch(sizes):
    lat = pltpu.VMEM((sizes.lat_rows, sizes.fy), jnp.float32)
    dep = pltpu.VMEM((sizes.dep_rows, sizes.fy), jnp.float32)
    return [lat, lat, dep, dep, pltpu.VMEM((-(-sizes.dep_fine // 8) * 8, sizes.cy), jnp.float32)]


def gather_scratch(sizes):
    return pltpu.VMEM((-(-5 * sizes.cx // 8) * 8, sizes.fy), jnp.float32)


def like(x):
    return jax.ShapeDtypeStruct(x.shape, x.dtype)


def call(kernel, name, smem, vmem, outs, scratch, work):
    moved = sum(x.size * 4 for x in vmem) + sum(4 * o.size for o in outs)
    return pl.pallas_call(
        kernel,
        name=name,
        out_shape=outs,
        in_specs=[SMEM] * len(smem) + [VMEM] * len(vmem),
        out_specs=[VMEM] * len(outs),
        scratch_shapes=scratch,
        compiler_params=pltpu.CompilerParams(vmem_limit_bytes=LIMIT),
        cost_estimate=pl.CostEstimate(flops=work, bytes_accessed=moved, transcendentals=0),
    )(*smem, *vmem)


def pack_stress(sizes, place, restrict, fine, coarse):
    def kernel(place, restrict, fine, coarse, latE, latO, depE, depO, diag, gather):
        send(sizes, place, fine, coarse, STRESS_X, STRESS_Z, restrict, latE, latO, depE, depO, diag, gather)

    return call(
        kernel, "pack_stress", (place, restrict), (fine, coarse), packs(sizes), [gather_scratch(sizes)], 10**6
    )


def materials(table, zone_fine, zone_coarse):
    def kernel(table, zone_fine, zone_coarse, fine, coarse):
        for zone_ref, out in ((zone_fine, fine), (zone_coarse, coarse)):

            def step(x, carry, zone_ref=zone_ref, out=out):
                zone = zone_ref[x]
                for column in range(7):
                    value = jnp.full(zone.shape, table[7, column])
                    for level in range(7):
                        value = jnp.where(zone == level, table[level, column], value)
                    out[column, x] = value
                return carry

            lax.fori_loop(0, zone_ref.shape[0], step, 0)

    outs = [jax.ShapeDtypeStruct((7,) + z.shape, jnp.float32) for z in (zone_fine, zone_coarse)]
    return call(kernel, "materials", (table,), (zone_fine, zone_coarse), outs, [], 5 * 10**6)


def velocity_step(sizes, place, interp, restrict, halos, fields, props, velocity):
    def kernel(
        place, interp, restrict, latE, latO, depE, depO, diag, sf, sc, pf, pc, vf, vc,
        of, oc, latE2, latO2, depE2, depO2, diag2, xlo, xhi, zlo, zhi, lift, gather,
    ):
        receive(sizes, place, latE, latO, depE, depO, diag, STRESS_Z, interp, xlo, xhi, zlo, zhi, lift)
        fine = Grid(sizes, True, sf, STRESS_X, STRESS_Z, xlo, xhi, zlo, zhi)
        velocity_rows(fine, vf, of, pf)
        coarse = Grid(sizes, False, sc, STRESS_X, STRESS_Z, xlo, xhi, zlo, zhi)
        velocity_rows(coarse, vc, oc, pc)
        send(sizes, place, of, oc, VELOCITY_X, VELOCITY_Z, restrict, latE2, latO2, depE2, depO2, diag2, gather)

    outs = [like(v) for v in velocity] + packs(sizes)
    out = call(
        kernel, "velocity_step", (place, interp, restrict), (*halos, *fields, *props, *velocity), outs,
        halo_scratch(sizes) + [gather_scratch(sizes)], 10**7,
    )
    return out[:2], out[2:]


def stress_step(sizes, place, interp, restrict, halos, velocity, props, stress, memory, again):
    def kernel(
        place, interp, restrict, latE, latO, depE, depO, diag, vf, vc, pf, pc, sf, sc, mf, mc,
        osf, osc, omf, omc, *rest,
    ):
        outgoing, (xlo, xhi, zlo, zhi, lift, gather) = rest[:-6], rest[-6:]
        receive(sizes, place, latE, latO, depE, depO, diag, VELOCITY_Z, interp, xlo, xhi, zlo, zhi, lift)
        fine = Grid(sizes, True, vf, VELOCITY_X, VELOCITY_Z, xlo, xhi, zlo, zhi)
        stress_rows(fine, sf, mf, osf, omf, pf)
        coarse = Grid(sizes, False, vc, VELOCITY_X, VELOCITY_Z, xlo, xhi, zlo, zhi)
        stress_rows(coarse, sc, mc, osc, omc, pc)
        if again:
            send(sizes, place, osf, osc, STRESS_X, STRESS_Z, restrict, *outgoing, gather)

    outs = [like(x) for x in (*stress, *memory)] + (packs(sizes) if again else [])
    out = call(
        kernel, "stress_step", (place, interp, restrict), (*halos, *velocity, *props, *stress, *memory), outs,
        halo_scratch(sizes) + [gather_scratch(sizes)], 2 * 10**7,
    )
    return out[:2], out[2:4], out[4:]


def rotation(low, high, pivot):
    gap = high - low
    twice = pivot + pivot
    square = twice * twice
    length2 = jnp.maximum(gap * gap + square, TINY)
    length = length2 * lax.rsqrt(length2)
    signed = jnp.where(gap >= 0, length, -length)
    middle = 0.5 * (low + high)
    reach = 0.5 * signed
    base = gap + signed

    def turn():
        inverse = lax.rsqrt(base * base + square)
        return base * inverse, twice * inverse

    return middle - reach, middle + reach, turn


def largest_eigenvalue(a, b, c, ab, ac, bc):
    a, b, turn = rotation(a, b, ab)
    cosine, sine = turn()
    ac, bc = cosine * ac - sine * bc, sine * ac + cosine * bc
    for sweep in range(3):
        if sweep > 0:
            a, b, turn = rotation(a, b, ab)
            cosine, sine = turn()
            ac, bc = cosine * ac, sine * ac
        a, c, turn = rotation(a, c, ac)
        cosine, sine = turn()
        ab, bc = -(sine * bc), cosine * bc
        b, c, turn = rotation(b, c, bc)
        if sweep < 2:
            cosine, sine = turn()
            ab, ac = cosine * ab, sine * ab
    return jnp.maximum(jnp.maximum(a, b), c)


def peaks(stress, props, peak):
    def kernel(sf, sc, pf, pc, kf, kc, of, oc):
        for s, p, k, o in ((sf, pf, kf, of), (sc, pc, kc, oc)):

            def step(x, carry, s=s, p=p, k=k, o=o):
                xx, yy, zz = s[0, x], s[1, x], s[2, x]
                top = largest_eigenvalue(xx, yy, zz, s[3, x], s[4, x], s[5, x])
                principal = (top - p[ISO, x] * (xx + yy + zz)) * p[SCALE, x]
                o[x] = jnp.maximum(k[x], principal)
                return carry

            lax.fori_loop(0, s.shape[1], step, 0)

    return call(kernel, "peaks", (), (*stress, *props, *peak), [like(k) for k in peak], [], 4 * 10**7)


def exchanged(arrays):
    latE, latO, depE, depO, diag = arrays
    lat, depth = lax.axis_size("lat"), lax.axis_size("depth")

    def swaps(count, first):
        pairs = [(i, (i + 1) % count) for i in range(first, count, 2)]
        return pairs + [(b, a) for a, b in pairs]

    across = [((i + 1) * depth, i * depth + depth - 1) for i in range(lat - 1)]
    diag = lax.ppermute(diag, ("lat", "depth"), across)
    depO = lax.ppermute(depO, "depth", swaps(depth, 1))
    depE = lax.ppermute(depE, "depth", swaps(depth, 0))
    latO = lax.ppermute(latO, "lat", swaps(lat, 1))
    latE = lax.ppermute(latE, "lat", swaps(lat, 0))
    return (latE, latO, depE, depO, diag)


def on_device(
    velocity_fine,
    stress_fine,
    memory_fine,
    peak_fine,
    zone_fine,
    velocity_coarse,
    stress_coarse,
    memory_coarse,
    peak_coarse,
    zone_coarse,
    zone_table,
    interp_weight,
    restrict_weight,
):
    sizes = Sizes(stress_fine.shape[1:], stress_coarse.shape[1:])
    place = jnp.stack(
        [
            lax.axis_index("lat"),
            lax.axis_index("depth"),
            jnp.int32(lax.axis_size("lat")),
            jnp.int32(lax.axis_size("depth")),
        ]
    ).astype(jnp.int32)
    buoyancy, lame, shear, decay, damping = [zone_table[:, i] for i in range(5)]
    table = jnp.stack(
        [
            buoyancy,
            lame,
            2.0 * shear,
            decay,
            damping * (1.0 - decay),
            lame / (3.0 * lame + 2.0 * shear),
            0.5 / shear,
        ],
        axis=1,
    )
    velocity = (velocity_fine, velocity_coarse)
    stress = (stress_fine, stress_coarse)
    memory = (memory_fine, memory_coarse)
    peak = (peak_fine, peak_coarse)
    outgoing = pack_stress(sizes, place, restrict_weight, *stress)
    props = materials(table, zone_fine, zone_coarse)
    for step in range(STEPS):
        halos = exchanged(outgoing)
        if step > 0:
            peak = peaks(stress, props, peak)
        velocity, outgoing = velocity_step(
            sizes, place, interp_weight, restrict_weight, halos, stress, props, velocity
        )
        halos = exchanged(outgoing)
        stress, memory, outgoing = stress_step(
            sizes, place, interp_weight, restrict_weight, halos, velocity, props, stress, memory, step + 1 < STEPS
        )
    peak = peaks(stress, props, peak)
    return (velocity[0], stress[0], memory[0], peak[0], velocity[1], stress[1], memory[1], peak[1])


def solution(mesh):
    field = P(None, "lat", "depth", None)
    scalar = P("lat", "depth", None)
    grid = (field, field, field, scalar)
    return jax.shard_map(
        on_device,
        mesh=mesh,
        in_specs=(*grid, scalar, *grid, scalar, P(), P(), P()),
        out_specs=(*grid, *grid),
        check_vma=False,
    )
```

profile of v0, /device:TPU:32, one launch (start us, length us, event | category | flops | bytes accessed | tf_op | source)
XLA Modules:
  0.0 110.6 jit_solution(6758137652705256547)
XLA Ops:
  0.6 0.0 copy-start.21
  0.7 0.1 pad_add_fusion.place
  0.7 1.5 %copy-done.3 = f32[6,12,16,384]{3,2,1,0:T(8,128)S(1)} copy-done((f32[6,12,16,384]{3,2,1,0:T(8,128)S(1)}, f32[6,12,16,384]{3,2,1,0:T(8,128)}, u32[]{:S(2)}) %copy-start.3) | copy-done | bytes 1769496
  2.2 1.0 copy-done.7
  3.2 0.7 copy-done.20
  3.9 1.3 %pack_stress.1 = (f32[144,384]{1,0:T(8,128)S(1)}, f32[144,384]{1,0:T(8,128)S(1)}, f32[72,384]{1,0:T(8,128)}, f32[72,384]{1,0:T(8,128)S(1)}, f32[8,128]{1,0:T(8,128)S(1)}) custom-call(s32[4]{0:T(128)S(1)} %pad_add_fusion.place, s32[2,3]{1,0:T(2,128)S(1)} %copy-done.20, f32[6,12,16,384]{3,2,1,0:T(8,128)S(1)} %copy-done.3, f32[6,4,32,128]{3,2,1,0:T(8,128)S(1)} %copy-done.7), custom_call_target="tpu_custom_call" | custom-call | flops 1000000 | bytes 2830336 | tf_op jit(solution)/shard_map/pack_stress/pallas_call | solution.py:376
  5.2 1.5 %collective-permute-start = (f32[144,384]{1,0:T(8,128)S(1)}, f32[144,384]{1,0:T(8,128)S(1)}, u32[]{:S(2)}, u32[]{:S(2)}) collective-permute-start(f32[144,384]{1,0:T(8,128)S(1)} %get-tuple-element.46), channel_id=1, source_target_pairs={{0,4},{8,12},{16,20},{24,28},{32,36},{40,44},{48,52},{56,60},{64,6... | collective-permute-start | bytes 663560 | tf_op jit(solution)/shard_map/ppermute | solution.py:524
  6.7 4.1 %collective-permute-start.1 = (f32[144,384]{1,0:T(8,128)S(1)}, f32[144,384]{1,0:T(8,128)S(1)}, u32[]{:S(2)}, u32[]{:S(2)}) collective-permute-start(f32[144,384]{1,0:T(8,128)S(1)} %get-tuple-element.47), channel_id=1, source_target_pairs={{4,8},{12,16},{20,24},{28,32},{36,40},{44,48},{52,56},{60,64},{68,... | collective-permute-start | bytes 663560 | tf_op jit(solution)/shard_map/ppermute | solution.py:523
  10.8 7.3 %collective-permute-start.3 = (f32[72,384]{1,0:T(8,128)S(1)}, f32[72,384]{1,0:T(8,128)S(1)}, u32[]{:S(2)}, u32[]{:S(2)}) collective-permute-start(f32[72,384]{1,0:T(8,128)S(1)} %get-tuple-element.49), channel_id=1, source_target_pairs={{1,2},{3,0},{2,1},{0,3},{5,6},{7,4},{6,5},{4,7},{9,10},{11,8},{10,... | collective-permute-start | bytes 331784 | tf_op jit(solution)/shard_map/ppermute | solution.py:521
  18.1 1.7 %collective-permute-start.4 = (f32[8,128]{1,0:T(8,128)S(1)}, f32[8,128]{1,0:T(8,128)S(1)}, u32[]{:S(2)}, u32[]{:S(2)}) collective-permute-start(f32[8,128]{1,0:T(8,128)S(1)} %get-tuple-element.50), channel_id=1, source_target_pairs={{4,3},{8,7},{12,11},{16,15},{20,19},{24,23},{28,27},{32,31},{36,35... | collective-permute-start | bytes 12296 | tf_op jit(solution)/shard_map/ppermute | solution.py:520
  19.8 0.1 slice_divide_fusion
  19.9 0.1 stack.19.table
  20.0 1.0 copy-done.15
  20.9 1.8 %materials.1 = (f32[7,12,16,384]{3,2,1,0:T(8,128)S(1)}, f32[7,4,32,128]{3,2,1,0:T(8,128)S(1)}) custom-call(f32[8,7]{1,0:T(8,128)S(1)} %stack.19.table, s32[12,16,384]{2,1,0:T(8,128)S(1)} %copy-done.15, s32[4,32,128]{2,1,0:T(8,128)S(1)} %copy-done.19), custom_call_target="tpu_custom_call" | custom-call | flops 5000000 | bytes 2883584 | tf_op jit(solution)/shard_map/materials/pallas_call | solution.py:376
  22.7 1.3 %copy-done = f32[7,12,16,384]{3,2,1,0:T(8,128)} copy-done((f32[7,12,16,384]{3,2,1,0:T(8,128)}, f32[7,12,16,384]{3,2,1,0:T(8,128)S(1)}, u32[]{:S(2)}) %copy-start) | copy-done | bytes 2064408
  24.1 0.0 collective-permute-done.4.diag
  24.1 1.2 %collective-permute-done.3.depO = f32[72,384]{1,0:T(8,128)S(1)} collective-permute-done((f32[72,384]{1,0:T(8,128)S(1)}, f32[72,384]{1,0:T(8,128)S(1)}, u32[]{:S(2)}, u32[]{:S(2)}) %collective-permute-start.3) | collective-permute-done | bytes 110624 | tf_op jit(solution)/shard_map/ppermute | solution.py:521
  25.4 0.0 copy-start.10
  25.4 1.2 %copy-done.10 = f32[3,12,16,384]{3,2,1,0:T(8,128)S(1)} copy-done((f32[3,12,16,384]{3,2,1,0:T(8,128)S(1)}, f32[3,12,16,384]{3,2,1,0:T(8,128)}, u32[]{:S(2)}) %copy-start.10) | copy-done | bytes 884760
  26.5 0.9 copy-done.16
  27.5 3.7 %velocity_step.2 = (f32[3,12,16,384]{3,2,1,0:T(8,128)S(1)}, f32[3,4,32,128]{3,2,1,0:T(8,128)S(1)}, f32[144,384]{1,0:T(8,128)S(1)}, f32[144,384]{1,0:T(8,128)S(1)...) custom-call(s32[4]{0:T(128)S(1)} %pad_add_fusion.place, s32[2,3]{1,0:T(2,128)S(1)} %copy-done.22, ...), custom_call_target="tpu_custom_call" | custom-call | flops 10000000 | bytes 8183808 | tf_op jit(solution)/shard_map/velocity_step/pallas_call | solution.py:376
  31.2 0.5 collective-permute-start.5
  31.7 1.4 %collective-permute-start.6 = (f32[144,384]{1,0:T(8,128)S(1)}, f32[144,384]{1,0:T(8,128)S(1)}, u32[]{:S(2)}, u32[]{:S(2)}) collective-permute-start(f32[144,384]{1,0:T(8,128)S(1)} %get-tuple-element.54), channel_id=1, source_target_pairs={{4,8},{12,16},{20,24},{28,32},{36,40},{44,48},{52,56},{60,64},{68,... | collective-permute-start | bytes 663560 | tf_op jit(solution)/shard_map/ppermute | solution.py:523
  33.1 0.9 collective-permute-start.7
  34.0 4.6 %collective-permute-start.8 = (f32[72,384]{1,0:T(8,128)S(1)}, f32[72,384]{1,0:T(8,128)S(1)}, u32[]{:S(2)}, u32[]{:S(2)}) collective-permute-start(f32[72,384]{1,0:T(8,128)S(1)} %get-tuple-element.56), channel_id=1, source_target_pairs={{1,2},{3,0},{2,1},{0,3},{5,6},{7,4},{6,5},{4,7},{9,10},{11,8},{10,... | collective-permute-start | bytes 331784 | tf_op jit(solution)/shard_map/ppermute | solution.py:521
  38.6 7.4 %collective-permute-start.9 = (f32[8,128]{1,0:T(8,128)S(1)}, f32[8,128]{1,0:T(8,128)S(1)}, u32[]{:S(2)}, u32[]{:S(2)}) collective-permute-start(f32[8,128]{1,0:T(8,128)S(1)} %get-tuple-element.57), channel_id=1, source_target_pairs={{4,3},{8,7},{12,11},{16,15},{20,19},{24,23},{28,27},{32,31},{36,35... | collective-permute-start | bytes 12296 | tf_op jit(solution)/shard_map/ppermute | solution.py:520
  46.0 1.3 %collective-permute-done.9.diag = f32[8,128]{1,0:T(8,128)S(1)} collective-permute-done((f32[8,128]{1,0:T(8,128)S(1)}, f32[8,128]{1,0:T(8,128)S(1)}, u32[]{:S(2)}, u32[]{:S(2)}) %collective-permute-start.9) | collective-permute-done | bytes 4128 | tf_op jit(solution)/shard_map/ppermute | solution.py:520
  47.3 0.0 collective-permute-done.7.depE
  47.3 0.0 collective-permute-done.8.depO
  47.3 0.0 collective-permute-done.5.latE
  47.3 6.9 %stress_step.2 = (f32[6,12,16,384]{3,2,1,0:T(8,128)}, f32[6,4,32,128]{3,2,1,0:T(8,128)S(1)}, f32[6,12,16,384]{3,2,1,0:T(8,128)}, f32[6,4,32,128]{3,2,1,0:T(8,128...) custom-call(s32[4]{0:T(128)S(1)} %pad_add_fusion.place, ...), custom_call_target="tpu_custom_call" | custom-call | flops 20000000 | bytes 13590528 | tf_op jit(solution)/shard_map/stress_step/pallas_call | solution.py:376
  54.2 0.0 collective-permute-start.10
  54.2 5.1 %collective-permute-start.11 = (f32[144,384]{1,0:T(8,128)S(1)}, f32[144,384]{1,0:T(8,128)S(1)}, u32[]{:S(2)}, u32[]{:S(2)}) collective-permute-start(f32[144,384]{1,0:T(8,128)S(1)} %get-tuple-element.61), channel_id=1, source_target_pairs={{4,8},{12,16},{20,24},{28,32},{36,40},{44,48},{52,56},{60,64},{68,... | collective-permute-start | bytes 663560 | tf_op jit(solution)/shard_map/ppermute | solution.py:523
  59.4 6.2 %collective-permute-start.13 = (f32[72,384]{1,0:T(8,128)S(1)}, f32[72,384]{1,0:T(8,128)S(1)}, u32[]{:S(2)}, u32[]{:S(2)}) collective-permute-start(f32[72,384]{1,0:T(8,128)S(1)} %get-tuple-element.63), channel_id=1, source_target_pairs={{1,2},{3,0},{2,1},{0,3},{5,6},{7,4},{6,5},{4,7},{9,10},{11,8},{10,... | collective-permute-start | bytes 331784 | tf_op jit(solution)/shard_map/ppermute | solution.py:521
  65.6 1.3 %collective-permute-start.14 = (f32[8,128]{1,0:T(8,128)S(1)}, f32[8,128]{1,0:T(8,128)S(1)}, u32[]{:S(2)}, u32[]{:S(2)}) collective-permute-start(f32[8,128]{1,0:T(8,128)S(1)} %get-tuple-element.64), channel_id=1, source_target_pairs={{4,3},{8,7},{12,11},{16,15},{20,19},{24,23},{28,27},{32,31},{36,35... | collective-permute-start | bytes 12296 | tf_op jit(solution)/shard_map/ppermute | solution.py:520
  66.9 1.3 %collective-permute-done.14.diag = f32[8,128]{1,0:T(8,128)S(1)} collective-permute-done((f32[8,128]{1,0:T(8,128)S(1)}, f32[8,128]{1,0:T(8,128)S(1)}, u32[]{:S(2)}, u32[]{:S(2)}) %collective-permute-start.14) | collective-permute-done | bytes 4128 | tf_op jit(solution)/shard_map/ppermute | solution.py:520
  68.2 5.7 %collective-permute-done.13.depO = f32[72,384]{1,0:T(8,128)S(1)} collective-permute-done((f32[72,384]{1,0:T(8,128)S(1)}, f32[72,384]{1,0:T(8,128)S(1)}, u32[]{:S(2)}, u32[]{:S(2)}) %collective-permute-start.13) | collective-permute-done | bytes 110624 | tf_op jit(solution)/shard_map/ppermute | solution.py:521
  73.9 0.0 collective-permute-done.10.latE
  73.9 1.5 %copy-done.5 = f32[6,12,16,384]{3,2,1,0:T(8,128)S(1)} copy-done((f32[6,12,16,384]{3,2,1,0:T(8,128)S(1)}, f32[6,12,16,384]{3,2,1,0:T(8,128)}, u32[]{:S(2)}) %copy-start.5) | copy-done | bytes 1769496
  75.4 5.0 %velocity_step.3 = (f32[3,12,16,384]{3,2,1,0:T(8,128)}, f32[3,4,32,128]{3,2,1,0:T(8,128)}, f32[144,384]{1,0:T(8,128)S(1)}, f32[144,384]{1,0:T(8,128)S(1)}, f32[7...) custom-call(s32[4]{0:T(128)S(1)} %pad_add_fusion.place, s32[2,3]{1,0:T(2,128)S(1)} %copy-done.22, ...), custom_call_target="tpu_custom_call" | custom-call | flops 10000000 | bytes 8183808 | tf_op jit(solution)/shard_map/velocity_step/pallas_call | solution.py:376
  80.4 0.1 collective-permute-start.16
  80.6 5.2 %collective-permute-start.18 = (f32[72,384]{1,0:T(8,128)S(1)}, f32[72,384]{1,0:T(8,128)S(1)}, u32[]{:S(2)}, u32[]{:S(2)}) collective-permute-start(f32[72,384]{1,0:T(8,128)S(1)} %get-tuple-element.71), channel_id=1, source_target_pairs={{1,2},{3,0},{2,1},{0,3},{5,6},{7,4},{6,5},{4,7},{9,10},{11,8},{10,... | collective-permute-start | bytes 331784 | tf_op jit(solution)/shard_map/ppermute | solution.py:521
  85.8 7.3 %collective-permute-start.19 = (f32[8,128]{1,0:T(8,128)S(1)}, f32[8,128]{1,0:T(8,128)S(1)}, u32[]{:S(2)}, u32[]{:S(2)}) collective-permute-start(f32[8,128]{1,0:T(8,128)S(1)} %get-tuple-element.72), channel_id=1, source_target_pairs={{4,3},{8,7},{12,11},{16,15},{20,19},{24,23},{28,27},{32,31},{36,35... | collective-permute-start | bytes 12296 | tf_op jit(solution)/shard_map/ppermute | solution.py:520
  93.1 4.0 %peaks.2 = (f32[12,16,384]{2,1,0:T(8,128)S(1)}, f32[4,32,128]{2,1,0:T(8,128)S(1)}) custom-call(f32[6,12,16,384]{3,2,1,0:T(8,128)S(1)} %copy-done.5, f32[6,4,32,128]{3,2,1,0:T(8,128)S(1)} %get-tuple-element.66.sc, f32[7,12,16,384]{3,2,1,0:T(8,128)S(1)} %copy-done.1, f32[7,4,32,128]{3,2,1,0:T(8,128)S(1)} %get-tuple-element.52.pc, ...), custom_call_target="tpu_custom_call" | custom-call | flops 40000000 | bytes 5406720 | tf_op jit(solution)/shard_map/peaks/pallas_call | solution.py:376
  97.1 6.4 %stress_step.3 = (f32[6,12,16,384]{3,2,1,0:T(8,128)}, f32[6,4,32,128]{3,2,1,0:T(8,128)}, f32[6,12,16,384]{3,2,1,0:T(8,128)}, f32[6,4,32,128]{3,2,1,0:T(8,128)}) custom-call(s32[4]{0:T(128)S(1)} %pad_add_fusion.place, s32[2,3]{1,0:T(2,128)S(1)} %copy-done.22, s32[2,3]{1,0:T(2,128)S(1)} %copy-done.21, f32[144,384]{1,0:T(8,128)S(1)} %collective-permute-done.15.latE, ...), custom_call_target="tpu_custom_call" | custom-call | flops 20000000 | bytes 12922880 | tf_op jit(solution)/shard_map/stress_step/pallas_call | solution.py:376
  103.6 1.5 %copy-done.9 = f32[6,12,16,384]{3,2,1,0:T(8,128)S(1)} copy-done((f32[6,12,16,384]{3,2,1,0:T(8,128)S(1)}, f32[6,12,16,384]{3,2,1,0:T(8,128)}, u32[]{:S(2)}) %copy-start.9) | copy-done | bytes 1769496
  105.0 1.0 copy-done.12
  106.0 4.6 %peaks.3 = (f32[12,16,384]{2,1,0:T(8,128)}, f32[4,32,128]{2,1,0:T(8,128)}) custom-call(f32[6,12,16,384]{3,2,1,0:T(8,128)S(1)} %copy-done.9, f32[6,4,32,128]{3,2,1,0:T(8,128)S(1)} %copy-done.12, f32[7,12,16,384]{3,2,1,0:T(8,128)S(1)} %copy-done.2, f32[7,4,32,128]{3,2,1,0:T(8,128)S(1)} %get-tuple-element.52.pc, f32[12,16,384]{2,1,0:T(8,128)S(1)} %get-tuple-element.79.kf, ...), custom_call_target="tpu_custom_call" | custom-call | flops 40000000 | bytes 5406720 | tf_op jit(solution)/shard_map/peaks/pallas_call | solution.py:376
  (51 shorter events, 0.1 us)
Async XLA Ops:
  0.6 24.7 %copy-start.21 = (s32[2,3]{1,0:T(2,128)S(1)}, s32[2,3]{1,0:T(2,128)}, u32[]{:S(2)}) copy-start(s32[2,3]{1,0:T(2,128)} %restrict.9) | copy-start | bytes 76
  0.6 19.2 %copy-start.23 = (f32[8,5]{1,0:T(8,128)S(1)}, f32[8,5]{1,0:T(8,128)}, u32[]{:S(2)}) copy-start(f32[8,5]{1,0:T(8,128)} %param.23) | copy-start | bytes 484
  0.7 24.7 %copy-start.22 = (s32[2,3]{1,0:T(2,128)S(1)}, s32[2,3]{1,0:T(2,128)}, u32[]{:S(2)}) copy-start(s32[2,3]{1,0:T(2,128)} %interp.7) | copy-start | bytes 76
  0.7 1.5 %copy-start.3 = (f32[6,12,16,384]{3,2,1,0:T(8,128)S(1)}, f32[6,12,16,384]{3,2,1,0:T(8,128)}, u32[]{:S(2)}) copy-start(f32[6,12,16,384]{3,2,1,0:T(8,128)} %sf.3) | copy-start | bytes 5308420
  2.2 1.0 copy-start.7
  3.2 0.7 copy-start.20
  3.9 16.1 %copy-start.19 = (s32[4,32,128]{2,1,0:T(8,128)S(1)}, s32[4,32,128]{2,1,0:T(8,128)}, u32[]{:S(2)}) copy-start(s32[4,32,128]{2,1,0:T(8,128)} %zone_coarse.1) | copy-start | bytes 196612
  3.9 21.4 %copy-start.4 = (f32[6,12,16,384]{3,2,1,0:T(8,128)S(1)}, f32[6,12,16,384]{3,2,1,0:T(8,128)}, u32[]{:S(2)}) copy-start(f32[6,12,16,384]{3,2,1,0:T(8,128)} %sf.3) | copy-start | bytes 5308420
  3.9 21.4 %copy-start.8 = (f32[6,4,32,128]{3,2,1,0:T(8,128)S(1)}, f32[6,4,32,128]{3,2,1,0:T(8,128)}, u32[]{:S(2)}) copy-start(f32[6,4,32,128]{3,2,1,0:T(8,128)} %sc.3) | copy-start | bytes 1179652
  5.2 20.1 %collective-permute-start = (f32[144,384]{1,0:T(8,128)S(1)}, f32[144,384]{1,0:T(8,128)S(1)}, u32[]{:S(2)}, u32[]{:S(2)}) collective-permute-start(f32[144,384]{1,0:T(8,128)S(1)} %get-tuple-element.46), channel_id=1, source_target_pairs={{0,4},{8,12},{16,20},{24,28},{32,36},{40,44},{48,52},{56,60},{64,6... | collective-permute-start | bytes 663560 | tf_op jit(solution)/shard_map/ppermute | solution.py:524
  6.7 18.6 %collective-permute-start.1 = (f32[144,384]{1,0:T(8,128)S(1)}, f32[144,384]{1,0:T(8,128)S(1)}, u32[]{:S(2)}, u32[]{:S(2)}) collective-permute-start(f32[144,384]{1,0:T(8,128)S(1)} %get-tuple-element.47), channel_id=1, source_target_pairs={{4,8},{12,16},{20,24},{28,32},{36,40},{44,48},{52,56},{60,64},{68,... | collective-permute-start | bytes 663560 | tf_op jit(solution)/shard_map/ppermute | solution.py:523
  10.8 13.3 %collective-permute-start.2 = (f32[72,384]{1,0:T(8,128)}, f32[72,384]{1,0:T(8,128)S(1)}, u32[]{:S(2)}, u32[]{:S(2)}) collective-permute-start(f32[72,384]{1,0:T(8,128)} %get-tuple-element.48), channel_id=1, source_target_pairs={{0,1},{2,3},{1,0},{3,2},{4,5},{6,7},{5,4},{7,6},{8,9},{10,11},{9,8... | collective-permute-start | bytes 331784 | tf_op jit(solution)/shard_map/ppermute | solution.py:522
  10.8 14.5 %collective-permute-start.3 = (f32[72,384]{1,0:T(8,128)S(1)}, f32[72,384]{1,0:T(8,128)S(1)}, u32[]{:S(2)}, u32[]{:S(2)}) collective-permute-start(f32[72,384]{1,0:T(8,128)S(1)} %get-tuple-element.49), channel_id=1, source_target_pairs={{1,2},{3,0},{2,1},{0,3},{5,6},{7,4},{6,5},{4,7},{9,10},{11,8},{10,... | collective-permute-start | bytes 331784 | tf_op jit(solution)/shard_map/ppermute | solution.py:521
  18.1 6.0 %collective-permute-start.4 = (f32[8,128]{1,0:T(8,128)S(1)}, f32[8,128]{1,0:T(8,128)S(1)}, u32[]{:S(2)}, u32[]{:S(2)}) collective-permute-start(f32[8,128]{1,0:T(8,128)S(1)} %get-tuple-element.50), channel_id=1, source_target_pairs={{4,3},{8,7},{12,11},{16,15},{20,19},{24,23},{28,27},{32,31},{36,35... | collective-permute-start | bytes 12296 | tf_op jit(solution)/shard_map/ppermute | solution.py:520
  20.0 1.0 copy-start.15
  22.7 1.3 %copy-start = (f32[7,12,16,384]{3,2,1,0:T(8,128)}, f32[7,12,16,384]{3,2,1,0:T(8,128)S(1)}, u32[]{:S(2)}) copy-start(f32[7,12,16,384]{3,2,1,0:T(8,128)S(1)} %get-tuple-element.51.pf) | copy-start | bytes 6193156
  25.4 1.2 %copy-start.10 = (f32[3,12,16,384]{3,2,1,0:T(8,128)S(1)}, f32[3,12,16,384]{3,2,1,0:T(8,128)}, u32[]{:S(2)}) copy-start(f32[3,12,16,384]{3,2,1,0:T(8,128)} %vf.1) | copy-start | bytes 2654212
  26.5 0.9 copy-start.16
  27.5 19.8 %copy-start.13 = (f32[6,4,32,128]{3,2,1,0:T(8,128)S(1)}, f32[6,4,32,128]{3,2,1,0:T(8,128)}, u32[]{:S(2)}) copy-start(f32[6,4,32,128]{3,2,1,0:T(8,128)} %mc.1) | copy-start | bytes 1179652
  31.2 16.1 %collective-permute-start.5 = (f32[144,384]{1,0:T(8,128)S(1)}, f32[144,384]{1,0:T(8,128)S(1)}, u32[]{:S(2)}, u32[]{:S(2)}) collective-permute-start(f32[144,384]{1,0:T(8,128)S(1)} %get-tuple-element.53), channel_id=1, source_target_pairs={{0,4},{8,12},{16,20},{24,28},{32,36},{40,44},{48,52},{56,60},{64,6... | collective-permute-start | bytes 663560 | tf_op jit(solution)/shard_map/ppermute | solution.py:524
  31.7 15.6 %collective-permute-start.6 = (f32[144,384]{1,0:T(8,128)S(1)}, f32[144,384]{1,0:T(8,128)S(1)}, u32[]{:S(2)}, u32[]{:S(2)}) collective-permute-start(f32[144,384]{1,0:T(8,128)S(1)} %get-tuple-element.54), channel_id=1, source_target_pairs={{4,8},{12,16},{20,24},{28,32},{36,40},{44,48},{52,56},{60,64},{68,... | collective-permute-start | bytes 663560 | tf_op jit(solution)/shard_map/ppermute | solution.py:523
  33.1 14.1 %collective-permute-start.7 = (f32[72,384]{1,0:T(8,128)S(1)}, f32[72,384]{1,0:T(8,128)S(1)}, u32[]{:S(2)}, u32[]{:S(2)}) collective-permute-start(f32[72,384]{1,0:T(8,128)S(1)} %get-tuple-element.55), channel_id=1, source_target_pairs={{0,1},{2,3},{1,0},{3,2},{4,5},{6,7},{5,4},{7,6},{8,9},{10,11},{9,8... | collective-permute-start | bytes 331784 | tf_op jit(solution)/shard_map/ppermute | solution.py:522
  34.0 13.3 %collective-permute-start.8 = (f32[72,384]{1,0:T(8,128)S(1)}, f32[72,384]{1,0:T(8,128)S(1)}, u32[]{:S(2)}, u32[]{:S(2)}) collective-permute-start(f32[72,384]{1,0:T(8,128)S(1)} %get-tuple-element.56), channel_id=1, source_target_pairs={{1,2},{3,0},{2,1},{0,3},{5,6},{7,4},{6,5},{4,7},{9,10},{11,8},{10,... | collective-permute-start | bytes 331784 | tf_op jit(solution)/shard_map/ppermute | solution.py:521
  38.6 8.7 %collective-permute-start.9 = (f32[8,128]{1,0:T(8,128)S(1)}, f32[8,128]{1,0:T(8,128)S(1)}, u32[]{:S(2)}, u32[]{:S(2)}) collective-permute-start(f32[8,128]{1,0:T(8,128)S(1)} %get-tuple-element.57), channel_id=1, source_target_pairs={{4,3},{8,7},{12,11},{16,15},{20,19},{24,23},{28,27},{32,31},{36,35... | collective-permute-start | bytes 12296 | tf_op jit(solution)/shard_map/ppermute | solution.py:520
  54.2 19.7 %collective-permute-start.10 = (f32[144,384]{1,0:T(8,128)S(1)}, f32[144,384]{1,0:T(8,128)S(1)}, u32[]{:S(2)}, u32[]{:S(2)}) collective-permute-start(f32[144,384]{1,0:T(8,128)S(1)} %get-tuple-element.60), channel_id=1, source_target_pairs={{0,4},{8,12},{16,20},{24,28},{32,36},{40,44},{48,52},{56,60},{64,6... | collective-permute-start | bytes 663560 | tf_op jit(solution)/shard_map/ppermute | solution.py:524
  54.2 19.7 %collective-permute-start.11 = (f32[144,384]{1,0:T(8,128)S(1)}, f32[144,384]{1,0:T(8,128)S(1)}, u32[]{:S(2)}, u32[]{:S(2)}) collective-permute-start(f32[144,384]{1,0:T(8,128)S(1)} %get-tuple-element.61), channel_id=1, source_target_pairs={{4,8},{12,16},{20,24},{28,32},{36,40},{44,48},{52,56},{60,64},{68,... | collective-permute-start | bytes 663560 | tf_op jit(solution)/shard_map/ppermute | solution.py:523
  59.3 8.8 %collective-permute-start.12 = (f32[72,384]{1,0:T(8,128)S(1)}, f32[72,384]{1,0:T(8,128)S(1)}, u32[]{:S(2)}, u32[]{:S(2)}) collective-permute-start(f32[72,384]{1,0:T(8,128)S(1)} %get-tuple-element.62), channel_id=1, source_target_pairs={{0,1},{2,3},{1,0},{3,2},{4,5},{6,7},{5,4},{7,6},{8,9},{10,11},{9,8... | collective-permute-start | bytes 331784 | tf_op jit(solution)/shard_map/ppermute | solution.py:522
  59.4 14.6 %collective-permute-start.13 = (f32[72,384]{1,0:T(8,128)S(1)}, f32[72,384]{1,0:T(8,128)S(1)}, u32[]{:S(2)}, u32[]{:S(2)}) collective-permute-start(f32[72,384]{1,0:T(8,128)S(1)} %get-tuple-element.63), channel_id=1, source_target_pairs={{1,2},{3,0},{2,1},{0,3},{5,6},{7,4},{6,5},{4,7},{9,10},{11,8},{10,... | collective-permute-start | bytes 331784 | tf_op jit(solution)/shard_map/ppermute | solution.py:521
  65.6 2.6 %collective-permute-start.14 = (f32[8,128]{1,0:T(8,128)S(1)}, f32[8,128]{1,0:T(8,128)S(1)}, u32[]{:S(2)}, u32[]{:S(2)}) collective-permute-start(f32[8,128]{1,0:T(8,128)S(1)} %get-tuple-element.64), channel_id=1, source_target_pairs={{4,3},{8,7},{12,11},{16,15},{20,19},{24,23},{28,27},{32,31},{36,35... | collective-permute-start | bytes 12296 | tf_op jit(solution)/shard_map/ppermute | solution.py:520
  73.9 1.5 %copy-start.5 = (f32[6,12,16,384]{3,2,1,0:T(8,128)S(1)}, f32[6,12,16,384]{3,2,1,0:T(8,128)}, u32[]{:S(2)}) copy-start(f32[6,12,16,384]{3,2,1,0:T(8,128)} %get-tuple-element.65.sf) | copy-start | bytes 5308420
  75.4 17.6 %copy-start.1 = (f32[7,12,16,384]{3,2,1,0:T(8,128)S(1)}, f32[7,12,16,384]{3,2,1,0:T(8,128)}, u32[]{:S(2)}) copy-start(f32[7,12,16,384]{3,2,1,0:T(8,128)} %copy-done) | copy-start | bytes 6193156
  75.4 17.6 %copy-start.14 = (f32[12,16,384]{2,1,0:T(8,128)S(1)}, f32[12,16,384]{2,1,0:T(8,128)}, u32[]{:S(2)}) copy-start(f32[12,16,384]{2,1,0:T(8,128)} %kf.1) | copy-start | bytes 884740
  75.4 17.6 %copy-start.18 = (f32[4,32,128]{2,1,0:T(8,128)S(1)}, f32[4,32,128]{2,1,0:T(8,128)}, u32[]{:S(2)}) copy-start(f32[4,32,128]{2,1,0:T(8,128)} %kc.1) | copy-start | bytes 196612
  80.4 16.7 %collective-permute-start.15 = (f32[144,384]{1,0:T(8,128)S(1)}, f32[144,384]{1,0:T(8,128)S(1)}, u32[]{:S(2)}, u32[]{:S(2)}) collective-permute-start(f32[144,384]{1,0:T(8,128)S(1)} %get-tuple-element.68), channel_id=1, source_target_pairs={{0,4},{8,12},{16,20},{24,28},{32,36},{40,44},{48,52},{56,60},{64,6... | collective-permute-start | bytes 663560 | tf_op jit(solution)/shard_map/ppermute | solution.py:524
  80.4 16.7 %collective-permute-start.16 = (f32[144,384]{1,0:T(8,128)S(1)}, f32[144,384]{1,0:T(8,128)S(1)}, u32[]{:S(2)}, u32[]{:S(2)}) collective-permute-start(f32[144,384]{1,0:T(8,128)S(1)} %get-tuple-element.69), channel_id=1, source_target_pairs={{4,8},{12,16},{20,24},{28,32},{36,40},{44,48},{52,56},{60,64},{68,... | collective-permute-start | bytes 663560 | tf_op jit(solution)/shard_map/ppermute | solution.py:523
  80.6 16.5 %collective-permute-start.17 = (f32[72,384]{1,0:T(8,128)S(1)}, f32[72,384]{1,0:T(8,128)S(1)}, u32[]{:S(2)}, u32[]{:S(2)}) collective-permute-start(f32[72,384]{1,0:T(8,128)S(1)} %get-tuple-element.70), channel_id=1, source_target_pairs={{0,1},{2,3},{1,0},{3,2},{4,5},{6,7},{5,4},{7,6},{8,9},{10,11},{9,8... | collective-permute-start | bytes 331784 | tf_op jit(solution)/shard_map/ppermute | solution.py:522
  80.6 16.5 %collective-permute-start.18 = (f32[72,384]{1,0:T(8,128)S(1)}, f32[72,384]{1,0:T(8,128)S(1)}, u32[]{:S(2)}, u32[]{:S(2)}) collective-permute-start(f32[72,384]{1,0:T(8,128)S(1)} %get-tuple-element.71), channel_id=1, source_target_pairs={{1,2},{3,0},{2,1},{0,3},{5,6},{7,4},{6,5},{4,7},{9,10},{11,8},{10,... | collective-permute-start | bytes 331784 | tf_op jit(solution)/shard_map/ppermute | solution.py:521
  85.8 11.4 %copy-start.6 = (f32[6,12,16,384]{3,2,1,0:T(8,128)S(1)}, f32[6,12,16,384]{3,2,1,0:T(8,128)}, u32[]{:S(2)}) copy-start(f32[6,12,16,384]{3,2,1,0:T(8,128)} %get-tuple-element.65.sf) | copy-start | bytes 5308420
  85.8 11.4 %copy-start.11 = (f32[3,12,16,384]{3,2,1,0:T(8,128)S(1)}, f32[3,12,16,384]{3,2,1,0:T(8,128)}, u32[]{:S(2)}) copy-start(f32[3,12,16,384]{3,2,1,0:T(8,128)} %get-tuple-element.38.vf) | copy-start | bytes 2654212
  85.8 11.4 %copy-start.17 = (f32[3,4,32,128]{3,2,1,0:T(8,128)S(1)}, f32[3,4,32,128]{3,2,1,0:T(8,128)}, u32[]{:S(2)}) copy-start(f32[3,4,32,128]{3,2,1,0:T(8,128)} %get-tuple-element.42.vc) | copy-start | bytes 589828
  85.8 11.3 %collective-permute-start.19 = (f32[8,128]{1,0:T(8,128)S(1)}, f32[8,128]{1,0:T(8,128)S(1)}, u32[]{:S(2)}, u32[]{:S(2)}) collective-permute-start(f32[8,128]{1,0:T(8,128)S(1)} %get-tuple-element.72), channel_id=1, source_target_pairs={{4,3},{8,7},{12,11},{16,15},{20,19},{24,23},{28,27},{32,31},{36,35... | collective-permute-start | bytes 12296 | tf_op jit(solution)/shard_map/ppermute | solution.py:520
  97.1 6.4 %copy-start.2 = (f32[7,12,16,384]{3,2,1,0:T(8,128)S(1)}, f32[7,12,16,384]{3,2,1,0:T(8,128)}, u32[]{:S(2)}) copy-start(f32[7,12,16,384]{3,2,1,0:T(8,128)} %copy-done) | copy-start | bytes 6193156
  103.6 1.5 %copy-start.9 = (f32[6,12,16,384]{3,2,1,0:T(8,128)S(1)}, f32[6,12,16,384]{3,2,1,0:T(8,128)}, u32[]{:S(2)}) copy-start(f32[6,12,16,384]{3,2,1,0:T(8,128)} %get-tuple-element.39.sf) | copy-start | bytes 5308420
  105.0 1.0 copy-start.12
where the time goes:
time: 111 us
  starting transfers between devices  54.6 us (49%)
  Pallas kernels  33.7 us (30%)
  local copies, waits for them, and re-layouts  11.6 us (10%)
  waiting for transfers between devices  9.65 us (9%)
    pallas_call x8, Pallas kernels, call(): pl.pallas_call(kernel, name=name, out_shape=outs, in_specs=[SMEM] * len(s...  33.7 us
    ppermute x4, starting transfers between devices, exchanged(): depO = lax.ppermute(depO, 'depth', swaps(depth, 1))  23.3 us
    ppermute x4, starting transfers between devices, exchanged(): diag = lax.ppermute(diag, ('lat', 'depth'), across)  17.6 us
    unnamed x48, local copies, waits for them, and re-layouts  11.5 us
    ppermute x4, starting transfers between devices, exchanged(): latO = lax.ppermute(latO, 'lat', swaps(lat, 1))  10.8 us
    ppermute x4, waiting for transfers between devices, exchanged(): depO = lax.ppermute(depO, 'depth', swaps(depth, 1))  6.99 us
    ppermute x4, waiting for transfers between devices, exchanged(): diag = lax.ppermute(diag, ('lat', 'depth'), across)  2.63 us
  transfers between devices with their start and end apart: 20, of which 4 were waited for; matrix products, arithmetic and copies ran while one was open for 0% of the time, Pallas kernels for 5%

commit v1 on v0

v1 whole, which is shorter than its diff:
```python
import functools

import jax
import jax.numpy as jnp
from jax import lax
from jax.experimental import pallas as pl
from jax.experimental.pallas import tpu as pltpu
from jax.sharding import PartitionSpec as P

STEPS = 2
DT = 0.4
NEAR = 9.0 / 8.0
FAR = 1.0 / 24.0
TINY = 1e-36

STRESS_X = ([(0, 1), (3, 2), (3, 1), (4, 2), (4, 1)], [(0, 0), (0, 1), (3, 0), (4, 0)])
STRESS_Z = ([(4, 2), (4, 1), (5, 2), (5, 1), (2, 1)], [(4, 0), (5, 0), (2, 0), (2, 1)])
VELOCITY_X = ([(0, 2), (0, 1), (1, 1), (2, 1)], [(0, 0), (1, 0), (1, 1), (2, 0), (2, 1)])
VELOCITY_Z = ([(2, 2), (2, 1), (0, 1), (1, 1)], [(2, 0), (0, 0), (0, 1), (1, 0), (1, 1)])

BULK = 2 * 10**6
CB, LAME, MU2, DECAY, DAMP, ISO, SCALE = range(7)


class Sizes:
    def __init__(self, fine, coarse):
        self.lats, self.depths = lax.axis_size("lat"), lax.axis_size("depth")
        self.fx, self.fz, self.fy = fine
        self.cx, self.cz, self.cy = coarse
        self.lanes = self.fy // self.cy
        self.lat_fine = 5 * self.fz
        self.lat_rows = self.lat_fine + -(-5 // self.lanes) * self.cz
        self.dep_fine = 5 * self.fx
        used = self.dep_fine + 5 * -(-self.cx // self.lanes)
        self.dep_rows = -(-used // 8) * 8

    def lat_slot(self, k):
        row = self.lat_fine + (k // self.lanes) * self.cz
        lane = (k % self.lanes) * self.cy
        return (slice(row, row + self.cz), slice(lane, lane + self.cy))

    def dep_slot(self, k, x):
        row = self.dep_fine + (x // self.lanes) * 5 + k
        lane = (x % self.lanes) * self.cy
        return (slice(row, row + 1), slice(lane, lane + self.cy))


def y_shift(f, offset, lane):
    width = f.shape[1]
    moved = pltpu.roll(f, (-offset) % width, 1)
    inside = lane < width - offset if offset > 0 else lane >= -offset
    return jnp.where(inside, moved, 0.0)


def z_shift(f, offset, row):
    depth = f.shape[0]
    moved = pltpu.roll(f, (-offset) % depth, 0)
    inside = row < depth - offset if offset > 0 else row >= -offset
    return jnp.where(inside, moved, 0.0)


def parts(at, up):
    def minus(a, b):
        if a is None or b is None:
            return a if b is None else -b
        return a - b

    if up:
        return minus(at(1), at(0)), minus(at(2), at(-1))
    return minus(at(0), at(-1)), minus(at(1), at(-2))


class Grid:
    def __init__(self, field, spacing):
        self.field, self.spacing = field, spacing
        _, self.nx, self.nz, self.ny = field.shape
        self.row = lax.broadcasted_iota(jnp.int32, (self.nz, self.ny), 0)
        self.lane = lax.broadcasted_iota(jnp.int32, (self.nz, self.ny), 1)

    def dx(self, comp, x, up):
        def at(offset):
            if isinstance(x, int) and not 0 <= x + offset < self.nx:
                return None
            return self.field[comp, x + offset]

        return parts(at, up)

    def dy(self, comp, x, up):
        f = self.field[comp, x]
        return parts(lambda offset: y_shift(f, offset, self.lane) if offset else f, up)

    def dz(self, comp, x, up):
        f = self.field[comp, x]
        return parts(lambda offset: z_shift(f, offset, self.row) if offset else f, up)


def over_rows(count, body):
    if count <= 8:
        for x in range(count):
            body(x)
        return

    def step(x, carry):
        body(x)
        return carry

    for x in (0, 1):
        body(x)
    lax.fori_loop(2, count - 2, step, 0)
    for x in (count - 2, count - 1):
        body(x)


def combine(*pairs):
    near = [p[0] for p in pairs if p[0] is not None]
    far = [p[1] for p in pairs if p[1] is not None]
    return NEAR * functools.reduce(jnp.add, near) - FAR * functools.reduce(jnp.add, far)


def velocity_rows(grid, velocity, out, props):
    scale = DT / grid.spacing

    def body(x):
        speed = scale * props[CB, x]
        ax = combine(grid.dx(0, x, True), grid.dy(3, x, False), grid.dz(4, x, False))
        out[0, x] = velocity[0, x] + speed * ax
        ay = combine(grid.dx(3, x, False), grid.dy(1, x, True), grid.dz(5, x, False))
        out[1, x] = velocity[1, x] + speed * ay
        az = combine(grid.dx(4, x, False), grid.dy(5, x, False), grid.dz(2, x, True))
        out[2, x] = velocity[2, x] + speed * az

    over_rows(grid.nx, body)


def stress_rows(grid, stress, memory, stress_out, memory_out, props):
    inverse = 1.0 / grid.spacing

    def body(x):
        lame, twice = props[LAME, x], props[MU2, x]
        decay, damp = props[DECAY, x], props[DAMP, x]
        if inverse != 1.0:
            lame, twice = lame * inverse, twice * inverse
        half = 0.5 * twice

        def finish(comp, rate):
            old = memory[comp, x]
            new = decay * old - damp * rate
            memory_out[comp, x] = new
            stress_out[comp, x] = stress[comp, x] + DT * (rate + 0.5 * (old + new))

        xx = combine(grid.dx(0, x, False))
        yy = combine(grid.dy(1, x, False))
        zz = combine(grid.dz(2, x, False))
        volume = lame * (xx + yy + zz)
        finish(0, volume + twice * xx)
        finish(1, volume + twice * yy)
        finish(2, volume + twice * zz)
        finish(3, half * combine(grid.dy(0, x, True), grid.dx(1, x, True)))
        finish(4, half * combine(grid.dz(0, x, True), grid.dx(2, x, True)))
        finish(5, half * combine(grid.dz(1, x, True), grid.dy(2, x, True)))

    over_rows(grid.nx, body)


class Edges:
    def __init__(self, sizes, fine, x_lists, z_lists, halo):
        self.sizes, self.fine = sizes, fine
        self.x_lists, self.z_lists = x_lists, z_lists
        self.xlo, self.xhi, self.zlo, self.zhi = halo
        self.nx, self.nz, self.ny = (
            (sizes.fx, sizes.fz, sizes.fy) if fine else (sizes.cx, sizes.cz, sizes.cy)
        )
        self.spacing = 1.0 if fine else 3.0
        self.row = lax.broadcasted_iota(jnp.int32, (8, self.ny), 0)

    def x_layer(self, ref, k):
        if self.fine:
            return ref[k * self.nz : (k + 1) * self.nz, :]
        return ref[self.sizes.lat_slot(k)]

    def low_x(self, comp, r):
        return self.x_layer(self.xlo, self.x_lists[0].index((comp, r)))

    def high_x(self, comp, r):
        return self.x_layer(self.xhi, self.x_lists[1].index((comp, r)))

    def dx(self, comp, x, up):
        if not isinstance(x, int):
            return None
        back = x - (self.nx - 1)
        if up:
            terms = {0: lambda: FAR * self.low_x(comp, 1)}
            ends = {
                0: lambda: NEAR * self.high_x(comp, 0) - FAR * self.high_x(comp, 1),
                -1: lambda: -FAR * self.high_x(comp, 0),
            }
        else:
            terms = {
                0: lambda: FAR * self.low_x(comp, 2) - NEAR * self.low_x(comp, 1),
                1: lambda: FAR * self.low_x(comp, 1),
            }
            ends = {0: lambda: -FAR * self.high_x(comp, 0)}
        found = [f() for f in (terms.get(x), ends.get(back)) if f is not None]
        return functools.reduce(jnp.add, found) if found else None

    def z_row(self, ref, k, x):
        if not self.fine:
            return ref[self.sizes.dep_slot(k, x)]
        if isinstance(x, int):
            return ref[k * self.nx + x : k * self.nx + x + 1, :]
        return ref[pl.ds(k * self.nx + x, 1), :]

    def dz(self, comp, x, up):
        low = {r: self.z_row(self.zlo, k, x) for k, (c, r) in enumerate(self.z_lists[0]) if c == comp}
        high = {r: self.z_row(self.zhi, k, x) for k, (c, r) in enumerate(self.z_lists[1]) if c == comp}
        row = self.row
        if up:
            top = jnp.where(row == 0, FAR * low[1], 0.0)
            bottom = jnp.where(
                row == 7, NEAR * high[0] - FAR * high[1], jnp.where(row == 6, -FAR * high[0], 0.0)
            )
        else:
            top = jnp.where(row == 0, FAR * low[2] - NEAR * low[1], jnp.where(row == 1, FAR * low[1], 0.0))
            bottom = jnp.where(row == 7, -FAR * high[0], 0.0)
        middle = [jnp.zeros((self.nz - 16, self.ny), jnp.float32)] if self.nz > 16 else []
        return jnp.concatenate([top, *middle, bottom], axis=0)


def total(*terms):
    found = [t for t in terms if t is not None]
    return functools.reduce(jnp.add, found) if found else None


def velocity_edges(edges, velocity, out, props):
    scale = DT / edges.spacing

    def body(x):
        speed = scale * props[CB, x]
        for comp, across, back, down, up in ((0, 0, True, 4, False), (1, 3, False, 5, False), (2, 4, False, 2, True)):
            added = total(edges.dx(across, x, back), edges.dz(down, x, up))
            out[comp, x] = velocity[comp, x] + speed * added

    over_rows(edges.nx, body)


def stress_edges(edges, stress, memory, stress_out, memory_out, props, then=None):
    inverse = 1.0 / edges.spacing

    def body(x):
        damp = props[DAMP, x]
        gain = DT - (0.5 * DT) * damp
        twice = inverse * props[MU2, x]
        half = 0.5 * twice

        def put(comp, rate):
            memory_out[comp, x] = memory[comp, x] if rate is None else memory[comp, x] - damp * rate
            stress_out[comp, x] = stress[comp, x] if rate is None else stress[comp, x] + gain * rate

        xx, zz = edges.dx(0, x, False), edges.dz(2, x, False)
        volume = inverse * props[LAME, x] * total(xx, zz)
        put(0, volume if xx is None else volume + twice * xx)
        put(1, volume)
        put(2, volume + twice * zz)
        xy = edges.dx(1, x, True)
        put(3, None if xy is None else half * xy)
        put(4, half * total(edges.dx(2, x, True), edges.dz(0, x, True)))
        put(5, half * edges.dz(1, x, True))
        if then is not None:
            then(x)

    over_rows(edges.nx, body)


def receive(sizes, halos, z_lists, interp, halo, lift):
    depO, diag, depE, latO, latE = halos
    xlo, xhi, zlo, zhi = halo
    lat, depth = lax.axis_index("lat"), lax.axis_index("depth")
    lat_even, depth_even = lax.rem(lat, 2) == 0, lax.rem(depth, 2) == 0
    last_lat, last_depth = sizes.lats - 1, sizes.depths - 1

    @pl.when(lat_even)
    def _():
        xlo[...] = latO[...]
        xhi[...] = latE[...]

    @pl.when(jnp.logical_not(lat_even))
    def _():
        xlo[...] = latE[...]
        xhi[...] = latO[...]

    @pl.when(lat == 0)
    def _():
        xlo[...] = jnp.zeros_like(xlo)

    @pl.when(lat == last_lat)
    def _():
        xhi[...] = jnp.zeros_like(xhi)

    @pl.when(depth_even)
    def _():
        zlo[...] = depO[...]
        zhi[...] = depE[...]

    @pl.when(jnp.logical_not(depth_even))
    def _():
        zlo[...] = depE[...]
        zhi[...] = depO[...]

    @pl.when(depth == 0)
    def _():
        zlo[0 : sizes.dep_fine, :] = jnp.zeros((sizes.dep_fine, sizes.fy), jnp.float32)

    @pl.when(depth == last_depth)
    def _():
        count = len(z_lists[1])
        lift[...] = jnp.zeros_like(lift)
        beyond = jnp.where(lat == last_lat, 0.0, 1.0)
        for k in range(count):
            planes = [depO[sizes.dep_slot(k, a)] for a in range(sizes.cx)]
            planes.append(diag[k : k + 1, :] * beyond)
            for a in range(sizes.cx):
                for p in range(3):
                    share = interp[0, p].astype(jnp.float32) * 0.125
                    x = k * sizes.fx + 3 * a + p
                    lift[x : x + 1, :] = share * planes[a] + (1.0 - share) * planes[a + 1]
        c = lax.broadcasted_iota(jnp.int32, (sizes.cy, sizes.fy), 0)
        f = lax.broadcasted_iota(jnp.int32, (sizes.cy, sizes.fy), 1)
        gap = f - 3 * c
        spread = jnp.zeros((sizes.cy, sizes.fy), jnp.float32)
        for p in range(3):
            share = interp[1, p].astype(jnp.float32) * 0.125
            spread = jnp.where(gap == p, share, spread)
            spread = jnp.where(gap == p - 3, 1.0 - share, spread)
        ghost = jnp.dot(
            lift[...], spread, precision=lax.Precision.HIGHEST, preferred_element_type=jnp.float32
        )
        zhi[...] = jnp.zeros_like(zhi)
        zhi[0 : sizes.dep_fine, :] = ghost[0 : sizes.dep_fine, :]


def send(sizes, fine, coarse, x_lists, z_lists, restrict, buffers, gather):
    depO, diag, depE, latO, latE = buffers
    lat, depth = lax.axis_index("lat"), lax.axis_index("depth")
    lat_even, depth_even = lax.rem(lat, 2) == 0, lax.rem(depth, 2) == 0
    last_depth = sizes.depths - 1

    def pack_x(up, down):
        for ref, entries, high in ((up, x_lists[0], True), (down, x_lists[1], False)):
            for k, (comp, r) in enumerate(entries):
                ref[k * sizes.fz : (k + 1) * sizes.fz, :] = fine[comp, sizes.fx - r if high else r]
                ref[sizes.lat_slot(k)] = coarse[comp, sizes.cx - r if high else r]

    def pack_z(up, down):
        for ref, entries, high in ((up, z_lists[0], True), (down, z_lists[1], False)):
            for k, (comp, r) in enumerate(entries):
                z = sizes.fz - r if high else r
                for x in range(sizes.fx):
                    ref[k * sizes.fx + x : k * sizes.fx + x + 1, :] = fine[comp, x, z : z + 1, :]
                z = sizes.cz - r if high else r
                for x in range(sizes.cx):
                    ref[sizes.dep_slot(k, x)] = coarse[comp, x, z : z + 1, :]

    @pl.when(lat_even)
    def _():
        pack_x(latE, latO)

    @pl.when(jnp.logical_not(lat_even))
    def _():
        pack_x(latO, latE)

    @pl.when(depth_even)
    def _():
        pack_z(depE, depO)

    @pl.when(jnp.logical_not(depth_even))
    def _():
        pack_z(depO, depE)

    diag[...] = jnp.zeros_like(diag)

    @pl.when(depth == 0)
    def _():
        for k, (comp, j) in enumerate(z_lists[1]):
            for x in range(sizes.cx):
                plane = ((2.0 - j) * coarse[comp, x, 0:1, :] + (1.0 + j) * coarse[comp, x, 1:2, :]) / 3.0
                depO[sizes.dep_slot(k, x)] = plane
                if x == 0:
                    diag[k : k + 1, :] = plane

    @pl.when(depth == last_depth)
    def _():
        wx = [restrict[0, p].astype(jnp.float32) for p in range(3)]
        wy = [restrict[1, p].astype(jnp.float32) for p in range(3)]
        gather[...] = jnp.zeros_like(gather)
        for k, (comp, r) in enumerate(z_lists[0]):
            z = sizes.fz - 3 * r
            for a in range(sizes.cx):
                total = None
                for p in range(3):
                    f = fine[comp, 3 * a + p, z : z + 3, :]
                    layers = wx[p] * (f[0:1] + f[1:2] + f[2:3])
                    total = layers if total is None else total + layers
                row = k * sizes.cx + a
                gather[row : row + 1, :] = total
        f = lax.broadcasted_iota(jnp.int32, (sizes.fy, sizes.cy), 0)
        c = lax.broadcasted_iota(jnp.int32, (sizes.fy, sizes.cy), 1)
        gap = f - 3 * c
        table = jnp.zeros((sizes.fy, sizes.cy), jnp.float32)
        for p in range(3):
            table = jnp.where(gap == p, wy[p], table)
        summed = jnp.dot(
            gather[...], table, precision=lax.Precision.HIGHEST, preferred_element_type=jnp.float32
        )
        norm = jnp.full((1, sizes.cy), 3.0 * (wx[0] + wx[1] + wx[2]) * (wy[0] + wy[1] + wy[2]))
        lifted = summed / norm
        for k in range(len(z_lists[0])):
            for a in range(sizes.cx):
                row = k * sizes.cx + a
                depO[sizes.dep_slot(k, a)] = lifted[row : row + 1, :]


SMEM = pl.BlockSpec(memory_space=pltpu.SMEM)
VMEM = pl.BlockSpec(memory_space=pltpu.VMEM)
HBM = pl.BlockSpec(memory_space=pltpu.HBM)
LIMIT = 24 * 1024 * 1024
PACK_LIMIT = 63 * 1024 * 1024
FIRST_LIMIT = 40 * 1024 * 1024


def packs(sizes):
    lat = jax.ShapeDtypeStruct((sizes.lat_rows, sizes.fy), jnp.float32)
    dep = jax.ShapeDtypeStruct((sizes.dep_rows, sizes.fy), jnp.float32)
    return [dep, jax.ShapeDtypeStruct((8, sizes.cy), jnp.float32), dep, lat, lat]


def halo_scratch(sizes):
    lat = pltpu.VMEM((sizes.lat_rows, sizes.fy), jnp.float32)
    dep = pltpu.VMEM((sizes.dep_rows, sizes.fy), jnp.float32)
    return [lat, lat, dep, dep, pltpu.VMEM((-(-sizes.dep_fine // 8) * 8, sizes.cy), jnp.float32)]


def gather_scratch(sizes):
    return pltpu.VMEM((-(-5 * sizes.cx // 8) * 8, sizes.fy), jnp.float32)


def like(x):
    return jax.ShapeDtypeStruct(x.shape, x.dtype)


def call(kernel, name, smem, vmem, outs, scratch, work, far=(), far_outs=(), limit=LIMIT):
    outs = [*far_outs, *outs]
    moved = sum(x.size * 4 for x in (*far, *vmem)) + sum(4 * o.size for o in outs)
    return pl.pallas_call(
        kernel,
        name=name,
        out_shape=outs,
        in_specs=[SMEM] * len(smem) + [HBM] * len(far) + [VMEM] * len(vmem),
        out_specs=[HBM] * len(far_outs) + [VMEM] * (len(outs) - len(far_outs)),
        scratch_shapes=scratch,
        compiler_params=pltpu.CompilerParams(vmem_limit_bytes=limit),
        cost_estimate=pl.CostEstimate(flops=work, bytes_accessed=moved, transcendentals=0),
    )(*smem, *far, *vmem)


def room(x):
    return pltpu.VMEM(x.shape, x.dtype)


def pack_stress(sizes, restrict, fine, coarse):
    def kernel(restrict, fine, coarse, *rest):
        buffers, (gather, near_fine, near_coarse, sems) = rest[:5], rest[5:]
        fx = sizes.fx
        copies = []
        for source, target, part in (
            (fine, near_fine, (slice(4, 6),)),
            (fine, near_fine, (2,)),
            (coarse, near_coarse, (slice(2, 6),)),
            (coarse, near_coarse, (0,)),
            (fine, near_fine, (0, slice(0, 2))),
            (fine, near_fine, (0, slice(fx - 1, fx))),
            (fine, near_fine, (3, slice(0, 1))),
            (fine, near_fine, (3, slice(fx - 2, fx))),
        ):
            copies.append(pltpu.make_async_copy(source.at[part], target.at[part], sems.at[len(copies)]))
        for copy in copies:
            copy.start()
        for copy in copies:
            copy.wait()
        send(sizes, near_fine, near_coarse, STRESS_X, STRESS_Z, restrict, buffers, gather)

    scratch = [gather_scratch(sizes), room(fine), room(coarse), pltpu.SemaphoreType.DMA((8,))]
    return call(
        kernel, "pack_stress", (restrict,), (), packs(sizes), scratch, 10**6, far=(fine, coarse), limit=PACK_LIMIT
    )


def material_rows(table, zone, out):
    def step(x, carry):
        kind = zone[x]
        for column in range(7):
            value = jnp.full(kind.shape, table[7, column])
            for level in range(7):
                value = jnp.where(kind == level, table[level, column], value)
            out[column, x] = value
        return carry

    lax.fori_loop(0, zone.shape[0], step, 0)


def first_bulk(table, zones, stress, velocity):
    def kernel(table, *rest):
        far, (of, oc, pf, pc), near, sems = rest[:6], rest[6:10], rest[10:16], rest[16]
        copies = [pltpu.make_async_copy(a, b, sems.at[i]) for i, (a, b) in enumerate(zip(far, near))]
        for copy in copies:
            copy.start()
        zf, zc, sf, sc, vf, vc = near
        copies[0].wait()
        material_rows(table, zf, pf)
        copies[1].wait()
        material_rows(table, zc, pc)
        for copy in copies[2:]:
            copy.wait()
        velocity_rows(Grid(sf, 1.0), vf, of, pf)
        velocity_rows(Grid(sc, 3.0), vc, oc, pc)

    outs = [like(v) for v in velocity]
    outs += [jax.ShapeDtypeStruct((7,) + z.shape, jnp.float32) for z in zones]
    far = (*zones, *stress, *velocity)
    scratch = [room(x) for x in far] + [pltpu.SemaphoreType.DMA((6,))]
    out = call(kernel, "first_bulk", (table,), (), outs, scratch, BULK, far=far, limit=FIRST_LIMIT)
    return out[:2], out[2:]


def velocity_bulk(stress, props, velocity, peak):
    def kernel(sf, sc, pf, pc, vf, vc, *rest):
        kf, kc, of, oc, okf, okc = rest
        velocity_rows(Grid(sf, 1.0), vf, of, pf)
        velocity_rows(Grid(sc, 3.0), vc, oc, pc)
        peak_rows(sf, pf, kf, okf)
        peak_rows(sc, pc, kc, okc)

    outs = [like(x) for x in (*velocity, *peak)]
    out = call(kernel, "velocity_bulk", (), (*stress, *props, *velocity, *peak), outs, [], BULK)
    return out[:2], out[2:]


def stress_bulk(velocity, props, stress, memory):
    def kernel(vf, vc, pf, pc, sf, sc, mf, mc, osf, osc, omf, omc):
        stress_rows(Grid(vf, 1.0), sf, mf, osf, omf, pf)
        stress_rows(Grid(vc, 3.0), sc, mc, osc, omc, pc)

    outs = [like(x) for x in (*stress, *memory)]
    return call(kernel, "stress_bulk", (), (*velocity, *props, *stress, *memory), outs, [], BULK)


def velocity_finish(sizes, interp, restrict, halos, props, velocity):
    def kernel(interp, restrict, *rest):
        halos, (pf, pc), (vf, vc), (of, oc), buffers = rest[:5], rest[5:7], rest[7:9], rest[9:11], rest[11:16]
        halo, (lift, gather) = rest[16:20], rest[20:]
        receive(sizes, halos, STRESS_Z, interp, halo, lift)
        velocity_edges(Edges(sizes, True, STRESS_X, STRESS_Z, halo), vf, of, pf)
        velocity_edges(Edges(sizes, False, STRESS_X, STRESS_Z, halo), vc, oc, pc)
        send(sizes, of, oc, VELOCITY_X, VELOCITY_Z, restrict, buffers, gather)

    outs = [like(v) for v in velocity] + packs(sizes)
    out = call(
        kernel, "velocity_finish", (interp, restrict), (*halos, *props, *velocity), outs,
        halo_scratch(sizes) + [gather_scratch(sizes)], 10**7,
    )
    return out[:2], out[2:]


def stress_finish(sizes, interp, restrict, halos, props, stress, memory):
    def kernel(interp, restrict, *rest):
        halos, (pf, pc), (sf, sc, mf, mc), (osf, osc, omf, omc) = rest[:5], rest[5:7], rest[7:11], rest[11:15]
        outgoing, halo, (lift, gather) = rest[15:20], rest[20:24], rest[24:]
        receive(sizes, halos, VELOCITY_Z, interp, halo, lift)
        stress_edges(Edges(sizes, True, VELOCITY_X, VELOCITY_Z, halo), sf, mf, osf, omf, pf)
        stress_edges(Edges(sizes, False, VELOCITY_X, VELOCITY_Z, halo), sc, mc, osc, omc, pc)
        send(sizes, osf, osc, STRESS_X, STRESS_Z, restrict, outgoing, gather)

    outs = [like(x) for x in (*stress, *memory)] + packs(sizes)
    out = call(
        kernel, "stress_finish", (interp, restrict), (*halos, *props, *stress, *memory), outs,
        halo_scratch(sizes) + [gather_scratch(sizes)], 2 * 10**7,
    )
    return out[:2], out[2:4], out[4:]


def last_finish(sizes, interp, halos, props, stress, memory, peak, velocity):
    def kernel(interp, *rest):
        halos, (pf, pc), (sf, sc, mf, mc), (kf, kc), speeds = rest[:5], rest[5:7], rest[7:11], rest[11:13], rest[13:15]
        outs, halo, lift = rest[15:23], rest[23:27], rest[27]
        near, sems = rest[28:34], rest[34]

        def whole(i):
            source = speeds[i] if i < 2 else near[i - 2]
            return pltpu.make_async_copy(source, outs[i], sems.at[i])

        for i in range(2):
            whole(i).start()
        receive(sizes, halos, VELOCITY_Z, interp, halo, lift)
        osf, osc, omf, omc, okf, okc = near

        def store(x):
            for i in (2, 4):
                pltpu.make_async_copy(near[i - 2].at[:, x], outs[i].at[:, x], sems.at[i]).start()

        stress_edges(Edges(sizes, True, VELOCITY_X, VELOCITY_Z, halo), sf, mf, osf, omf, pf, store)
        stress_edges(Edges(sizes, False, VELOCITY_X, VELOCITY_Z, halo), sc, mc, osc, omc, pc)
        for i in (3, 5):
            whole(i).start()
        peak_rows(osf, pf, kf, okf)
        whole(6).start()
        peak_rows(osc, pc, kc, okc)
        whole(7).start()
        for i in range(8):
            whole(i).wait()

    outs = [like(x) for x in (*velocity, *stress, *memory, *peak)]
    scratch = halo_scratch(sizes) + [room(x) for x in (*stress, *memory, *peak)] + [pltpu.SemaphoreType.DMA((8,))]
    out = call(
        kernel, "last_finish", (interp,), (*halos, *props, *stress, *memory, *peak, *velocity), [],
        scratch, 2 * 10**7, far_outs=outs,
    )
    return out[:2], out[2:4], out[4:6], out[6:]


def rotation(low, high, pivot):
    gap = high - low
    twice = pivot + pivot
    square = twice * twice
    length2 = jnp.maximum(gap * gap + square, TINY)
    length = length2 * lax.rsqrt(length2)
    signed = jnp.where(gap >= 0, length, -length)
    middle = 0.5 * (low + high)
    reach = 0.5 * signed
    base = gap + signed

    def turn():
        inverse = lax.rsqrt(base * base + square)
        return base * inverse, twice * inverse

    return middle - reach, middle + reach, turn


def largest_eigenvalue(a, b, c, ab, ac, bc):
    a, b, turn = rotation(a, b, ab)
    cosine, sine = turn()
    ac, bc = cosine * ac - sine * bc, sine * ac + cosine * bc
    for sweep in range(3):
        if sweep > 0:
            a, b, turn = rotation(a, b, ab)
            cosine, sine = turn()
            ac, bc = cosine * ac, sine * ac
        a, c, turn = rotation(a, c, ac)
        cosine, sine = turn()
        ab, bc = -(sine * bc), cosine * bc
        b, c, turn = rotation(b, c, bc)
        if sweep < 2:
            cosine, sine = turn()
            ab, ac = cosine * ab, sine * ab
    return jnp.maximum(jnp.maximum(a, b), c)


def peak_rows(stress, props, peak, out, width=2):
    def step(i, carry):
        x = pl.ds(i * width, width)
        xx, yy, zz, xy, xz, yz = [stress[comp, x] for comp in range(6)]
        top = largest_eigenvalue(xx, yy, zz, xy, xz, yz)
        principal = (top - props[ISO, x] * (xx + yy + zz)) * props[SCALE, x]
        out[x] = jnp.maximum(peak[x], principal)
        return carry

    lax.fori_loop(0, stress.shape[1] // width, step, 0)


def exchanged(arrays):
    depO, diag, depE, latO, latE = arrays
    lat, depth = lax.axis_size("lat"), lax.axis_size("depth")

    def swaps(count, first):
        pairs = [(i, (i + 1) % count) for i in range(first, count, 2)]
        return pairs + [(b, a) for a, b in pairs]

    across = [((i + 1) * depth, i * depth + depth - 1) for i in range(lat - 1)]
    depO = lax.ppermute(depO, "depth", swaps(depth, 1))
    diag = lax.ppermute(diag, ("lat", "depth"), across)
    depE = lax.ppermute(depE, "depth", swaps(depth, 0))
    latO = lax.ppermute(latO, "lat", swaps(lat, 1))
    latE = lax.ppermute(latE, "lat", swaps(lat, 0))
    return (depO, diag, depE, latO, latE)


def on_device(
    velocity_fine,
    stress_fine,
    memory_fine,
    peak_fine,
    zone_fine,
    velocity_coarse,
    stress_coarse,
    memory_coarse,
    peak_coarse,
    zone_coarse,
    zone_table,
    interp_weight,
    restrict_weight,
):
    sizes = Sizes(stress_fine.shape[1:], stress_coarse.shape[1:])
    buoyancy, lame, shear, decay, damping = [zone_table[:, i] for i in range(5)]
    table = jnp.stack(
        [
            buoyancy,
            lame,
            2.0 * shear,
            decay,
            damping * (1.0 - decay),
            lame / (3.0 * lame + 2.0 * shear),
            0.5 / shear,
        ],
        axis=1,
    )
    velocity = (velocity_fine, velocity_coarse)
    stress = (stress_fine, stress_coarse)
    memory = (memory_fine, memory_coarse)
    peak = (peak_fine, peak_coarse)
    outgoing = pack_stress(sizes, restrict_weight, *stress)
    for step in range(STEPS):
        halos = exchanged(outgoing)
        if step == 0:
            velocity, props = first_bulk(table, (zone_fine, zone_coarse), stress, velocity)
        else:
            velocity, peak = velocity_bulk(stress, props, velocity, peak)
        velocity, outgoing = velocity_finish(
            sizes, interp_weight, restrict_weight, halos, props, velocity
        )
        halos = exchanged(outgoing)
        bulk = stress_bulk(velocity, props, stress, memory)
        if step + 1 < STEPS:
            stress, memory, outgoing = stress_finish(
                sizes, interp_weight, restrict_weight, halos, props, bulk[:2], bulk[2:]
            )
        else:
            velocity, stress, memory, peak = last_finish(
                sizes, interp_weight, halos, props, bulk[:2], bulk[2:], peak, velocity
            )
    return (velocity[0], stress[0], memory[0], peak[0], velocity[1], stress[1], memory[1], peak[1])


def solution(mesh):
    field = P(None, "lat", "depth", None)
    scalar = P("lat", "depth", None)
    grid = (field, field, field, scalar)
    return jax.shard_map(
        on_device,
        mesh=mesh,
        in_specs=(*grid, scalar, *grid, scalar, P(), P(), P()),
        out_specs=(*grid, *grid),
        check_vma=False,
    )
```

time: 111 us -> 92 us (0.83)
  the two profiles are of different devices: /device:TPU:32 before, /device:TPU:4 now
where the time goes in v1:
time: 92 us; the launch traced here: 91.2 us
  starting transfers between devices  60.5 us (66%)
  Pallas kernels  26.6 us (29%)
  local copies, waits for them, and re-layouts  2.77 us (3%)
  between operations  1.21 us (1%)
    ppermute x4, starting transfers between devices, exchanged(): diag = lax.ppermute(diag, ('lat', 'depth'), across)  36 us
    pallas_call x9, Pallas kernels, call(): pl.pallas_call(kernel, name=name, out_shape=outs, in_specs=[SMEM] * len(s...  26.6 us
    ppermute x4, starting transfers between devices, exchanged(): depO = lax.ppermute(depO, 'depth', swaps(depth, 1))  13.3 us
    ppermute x4, starting transfers between devices, exchanged(): latO = lax.ppermute(latO, 'lat', swaps(lat, 1))  5.95 us
    ppermute x4, starting transfers between devices, exchanged(): latE = lax.ppermute(latE, 'lat', swaps(lat, 0))  4.54 us
    unnamed x26, local copies, waits for them, and re-layouts  2.69 us
  transfers between devices with their start and end apart: 20, of which 0 were waited for; matrix products, arithmetic and copies ran while one was open for 0% of the time, Pallas kernels for 16%

profile of v1, /device:TPU:4, one launch (start us, length us, event | category | flops | bytes accessed | tf_op | source)
XLA Modules:
  0.0 91.2 jit_solution(11294103947258387848)
XLA Ops:
  0.7 3.1 %pack_stress.1 = (f32[72,384]{1,0:T(8,128)}, f32[8,128]{1,0:T(8,128)}, f32[72,384]{1,0:T(8,128)}, f32[144,384]{1,0:T(8,128)}, f32[144,384]{1,0:T(8,128)}) custom-call(s32[2,3]{1,0:T(2,128)} %restrict.7, f32[6,12,16,384]{3,2,1,0:T(8,128)} %sf.1, f32[6,4,32,128]{3,2,1,0:T(8,128)} %sc.1), custom_call_target="tpu_custom_call" | custom-call | flops 1000000 | bytes 2830336 | tf_op jit(solution)/shard_map/pack_stress/pallas_call | solution.py:453
  3.8 9.0 %collective-permute-start.1 = (f32[8,128]{1,0:T(8,128)}, f32[8,128]{1,0:T(8,128)S(1)}, u32[]{:S(2)}, u32[]{:S(2)}) collective-permute-start(f32[8,128]{1,0:T(8,128)} %get-tuple-element.61), channel_id=1, source_target_pairs={{4,3},{8,7},{12,11},{16,15},{20,19},{24,23},{28,27},{32,31},{36,35... | collective-permute-start | bytes 12296 | tf_op jit(solution)/shard_map/ppermute | solution.py:688
  12.7 0.1 collective-permute-start
  12.8 0.1 collective-permute-start.2
  12.9 0.6 collective-permute-start.3
  13.6 4.3 %collective-permute-start.4 = (f32[144,384]{1,0:T(8,128)}, f32[144,384]{1,0:T(8,128)S(1)}, u32[]{:S(2)}, u32[]{:S(2)}) collective-permute-start(f32[144,384]{1,0:T(8,128)} %get-tuple-element.64), channel_id=1, source_target_pairs={{0,4},{8,12},{16,20},{24,28},{32,36},{40,44},{48,52},{56,60},{64,6... | collective-permute-start | bytes 663560 | tf_op jit(solution)/shard_map/ppermute | solution.py:691
  17.8 0.1 slice_divide_fusion
  17.9 0.1 stack.2.table
  18.0 0.0 copy-start
  18.0 1.5 %copy-done = f32[6,12,16,384]{3,2,1,0:T(8,128)S(1)} copy-done((f32[6,12,16,384]{3,2,1,0:T(8,128)S(1)}, f32[6,12,16,384]{3,2,1,0:T(8,128)}, u32[]{:S(2)}) %copy-start) | copy-done | bytes 1769496
  19.5 1.2 %copy-done.3 = f32[3,12,16,384]{3,2,1,0:T(8,128)S(1)} copy-done((f32[3,12,16,384]{3,2,1,0:T(8,128)S(1)}, f32[3,12,16,384]{3,2,1,0:T(8,128)}, u32[]{:S(2)}) %copy-start.3) | copy-done | bytes 884760
  20.7 4.7 %first_bulk.1 = (f32[3,12,16,384]{3,2,1,0:T(8,128)S(1)}, f32[3,4,32,128]{3,2,1,0:T(8,128)S(1)}, f32[7,12,16,384]{3,2,1,0:T(8,128)S(1)}, f32[7,4,32,128]{3,2,1,0:T(8,128)S(1)}) custom-call(f32[8,7]{1,0:T(8,128)S(1)} %stack.2.table, s32[12,16,384]{2,1,0:T(8,128)S(1)} %copy-done.6, s32[4,32,128]{2,1,0:T(8,128)S(1)} %copy-done.8, ...), custom_call_target="tpu_custom_call" | custom-call | flops 2000000 | bytes 7208960 | tf_op jit(solution)/shard_map/first_bulk/pallas_call | solution.py:453
  25.3 0.0 collective-permute-done.1.rest_1_
  25.4 0.0 collective-permute-done.3.rest_3_
  25.4 0.0 copy-start.2
  25.4 0.0 copy-start.4
  25.4 1.1 %velocity_finish.2 = (f32[3,12,16,384]{3,2,1,0:T(8,128)S(1)}, f32[3,4,32,128]{3,2,1,0:T(8,128)S(1)}, f32[72,384]{1,0:T(8,128)S(1)}, f32[8,128]{1,0:T(8,128)S(1)}...) custom-call(s32[2,3]{1,0:T(2,128)S(1)} %copy-done.11, s32[2,3]{1,0:T(2,128)S(1)} %copy-done.10, ...), custom_call_target="tpu_custom_call" | custom-call | flops 10000000 | bytes 6021120 | tf_op jit(solution)/shard_map/velocity_finish/pallas_call | solution.py:453
  26.5 3.2 %collective-permute-start.8 = (f32[144,384]{1,0:T(8,128)S(1)}, f32[144,384]{1,0:T(8,128)S(1)}, u32[]{:S(2)}, u32[]{:S(2)}) collective-permute-start(f32[144,384]{1,0:T(8,128)S(1)} %get-tuple-element.72), channel_id=1, source_target_pairs={{4,8},{12,16},{20,24},{28,32},{36,40},{44,48},{52,56},{60,64},{68,... | collective-permute-start | bytes 663560 | tf_op jit(solution)/shard_map/ppermute | solution.py:690
  29.8 5.4 %collective-permute-start.5 = (f32[72,384]{1,0:T(8,128)S(1)}, f32[72,384]{1,0:T(8,128)S(1)}, u32[]{:S(2)}, u32[]{:S(2)}) collective-permute-start(f32[72,384]{1,0:T(8,128)S(1)} %get-tuple-element.69), channel_id=1, source_target_pairs={{1,2},{3,0},{2,1},{0,3},{5,6},{7,4},{6,5},{4,7},{9,10},{11,8},{10,... | collective-permute-start | bytes 331784 | tf_op jit(solution)/shard_map/ppermute | solution.py:687
  35.2 0.6 collective-permute-start.7
  35.7 8.6 %collective-permute-start.6 = (f32[8,128]{1,0:T(8,128)S(1)}, f32[8,128]{1,0:T(8,128)S(1)}, u32[]{:S(2)}, u32[]{:S(2)}) collective-permute-start(f32[8,128]{1,0:T(8,128)S(1)} %get-tuple-element.70), channel_id=1, source_target_pairs={{4,3},{8,7},{12,11},{16,15},{20,19},{24,23},{28,27},{32,31},{36,35... | collective-permute-start | bytes 12296 | tf_op jit(solution)/shard_map/ppermute | solution.py:688
  44.4 2.2 %stress_bulk.2 = (f32[6,12,16,384]{3,2,1,0:T(8,128)S(1)}, f32[6,4,32,128]{3,2,1,0:T(8,128)S(1)}, f32[6,12,16,384]{3,2,1,0:T(8,128)S(1)}, f32[6,4,32,128]{3,2,1,0:T(8,128)S(1)}) custom-call(f32[3,12,16,384]{3,2,1,0:T(8,128)S(1)} %get-tuple-element.74.vf, f32[3,4,32,128]{3,2,1,0:T(8,128)S(1)} %get-tuple-element.75.vc, ...), custom_call_target="tpu_custom_call" | custom-call | flops 2000000 | bytes 12255232 | tf_op jit(solution)/shard_map/stress_bulk/pallas_call | solution.py:453
  46.6 0.0 collective-permute-done.6.rest_1_
  46.6 0.0 collective-permute-done.7.rest_2_
  46.6 0.0 collective-permute-done.8.rest_3_
  46.6 0.0 copy-start.5
  46.7 0.0 copy-start.9
  46.7 1.4 %stress_finish.1 = (f32[6,12,16,384]{3,2,1,0:T(8,128)S(1)}, f32[6,4,32,128]{3,2,1,0:T(8,128)S(1)}, f32[6,12,16,384]{3,2,1,0:T(8,128)S(1)}, f32[6,4,32,128]{3,2,1...) custom-call(s32[2,3]{1,0:T(2,128)S(1)} %copy-done.11, ...), custom_call_target="tpu_custom_call" | custom-call | flops 20000000 | bytes 12509184 | tf_op jit(solution)/shard_map/stress_finish/pallas_call | solution.py:453
  48.1 1.7 %collective-permute-start.13 = (f32[144,384]{1,0:T(8,128)S(1)}, f32[144,384]{1,0:T(8,128)S(1)}, u32[]{:S(2)}, u32[]{:S(2)}) collective-permute-start(f32[144,384]{1,0:T(8,128)S(1)} %get-tuple-element.83), channel_id=1, source_target_pairs={{4,8},{12,16},{20,24},{28,32},{36,40},{44,48},{52,56},{60,64},{68,... | collective-permute-start | bytes 663560 | tf_op jit(solution)/shard_map/ppermute | solution.py:690
  49.8 0.0 collective-permute-start.14
  49.8 5.0 %collective-permute-start.10 = (f32[72,384]{1,0:T(8,128)S(1)}, f32[72,384]{1,0:T(8,128)S(1)}, u32[]{:S(2)}, u32[]{:S(2)}) collective-permute-start(f32[72,384]{1,0:T(8,128)S(1)} %get-tuple-element.80), channel_id=1, source_target_pairs={{1,2},{3,0},{2,1},{0,3},{5,6},{7,4},{6,5},{4,7},{9,10},{11,8},{10,... | collective-permute-start | bytes 331784 | tf_op jit(solution)/shard_map/ppermute | solution.py:687
  54.8 0.0 collective-permute-start.12
  54.9 7.7 %collective-permute-start.11 = (f32[8,128]{1,0:T(8,128)S(1)}, f32[8,128]{1,0:T(8,128)S(1)}, u32[]{:S(2)}, u32[]{:S(2)}) collective-permute-start(f32[8,128]{1,0:T(8,128)S(1)} %get-tuple-element.81), channel_id=1, source_target_pairs={{4,3},{8,7},{12,11},{16,15},{20,19},{24,23},{28,27},{32,31},{36,35... | collective-permute-start | bytes 12296 | tf_op jit(solution)/shard_map/ppermute | solution.py:688
  62.6 5.3 %velocity_bulk.1 = (f32[3,12,16,384]{3,2,1,0:T(8,128)S(1)}, f32[3,4,32,128]{3,2,1,0:T(8,128)S(1)}, f32[12,16,384]{2,1,0:T(8,128)S(1)}, f32[4,32,128]{2,1,0:T(8,128)S(1)}) custom-call(f32[6,12,16,384]{3,2,1,0:T(8,128)S(1)} %get-tuple-element.85.sf, f32[6,4,32,128]{3,2,1,0:T(8,128)S(1)} %get-tuple-element.86.sc, ...), custom_call_target="tpu_custom_call" | custom-call | flops 2000000 | bytes 7569408 | tf_op jit(solution)/shard_map/velocity_bulk/pallas_call | solution.py:453
  67.9 0.0 collective-permute-done.11.rest_1_
  67.9 0.0 collective-permute-done.10.rest_0_
  67.9 0.0 collective-permute-done.13.rest_3_
  67.9 0.0 collective-permute-done.14.rest_4_
  67.9 1.1 %velocity_finish.3 = (f32[3,12,16,384]{3,2,1,0:T(8,128)S(1)}, f32[3,4,32,128]{3,2,1,0:T(8,128)S(1)}, f32[72,384]{1,0:T(8,128)S(1)}, f32[8,128]{1,0:T(8,128)S(1)}...) custom-call(s32[2,3]{1,0:T(2,128)S(1)} %copy-done.11, s32[2,3]{1,0:T(2,128)S(1)} %copy-done.10, ...), custom_call_target="tpu_custom_call" | custom-call | flops 10000000 | bytes 6021120 | tf_op jit(solution)/shard_map/velocity_finish/pallas_call | solution.py:453
  69.0 0.4 collective-permute-start.18
  69.4 0.3 collective-permute-start.19
  69.7 2.8 %collective-permute-start.15 = (f32[72,384]{1,0:T(8,128)S(1)}, f32[72,384]{1,0:T(8,128)S(1)}, u32[]{:S(2)}, u32[]{:S(2)}) collective-permute-start(f32[72,384]{1,0:T(8,128)S(1)} %get-tuple-element.89), channel_id=1, source_target_pairs={{1,2},{3,0},{2,1},{0,3},{5,6},{7,4},{6,5},{4,7},{9,10},{11,8},{10,... | collective-permute-start | bytes 331784 | tf_op jit(solution)/shard_map/ppermute | solution.py:687
  72.5 0.0 collective-permute-start.17
  72.5 10.7 %collective-permute-start.16 = (f32[8,128]{1,0:T(8,128)S(1)}, f32[8,128]{1,0:T(8,128)S(1)}, u32[]{:S(2)}, u32[]{:S(2)}) collective-permute-start(f32[8,128]{1,0:T(8,128)S(1)} %get-tuple-element.90), channel_id=1, source_target_pairs={{4,3},{8,7},{12,11},{16,15},{20,19},{24,23},{28,27},{32,31},{36,35... | collective-permute-start | bytes 12296 | tf_op jit(solution)/shard_map/ppermute | solution.py:688
  83.2 2.2 %stress_bulk.3 = (f32[6,12,16,384]{3,2,1,0:T(8,128)S(1)}, f32[6,4,32,128]{3,2,1,0:T(8,128)S(1)}, f32[6,12,16,384]{3,2,1,0:T(8,128)S(1)}, f32[6,4,32,128]{3,2,1,0:T(8,128)S(1)}) custom-call(f32[3,12,16,384]{3,2,1,0:T(8,128)S(1)} %get-tuple-element.94.vf.rest_13_, f32[3,4,32,128]{3,2,1,0:T(8,128)S(1)} %get-tuple-element.95.vc.rest_14_, ...), custom_call_target="tpu_custom_call" | custom-call | flops 2000000 | bytes 12255232 | tf_op jit(solution)/shard_map/stress_bulk/pallas_call | solution.py:453
  85.5 0.0 collective-permute-done.15.rest_0_
  85.5 0.0 collective-permute-done.17.rest_2_
  85.5 5.5 %last_finish.1 = (f32[3,12,16,384]{3,2,1,0:T(8,128)}, f32[3,4,32,128]{3,2,1,0:T(8,128)}, f32[6,12,16,384]{3,2,1,0:T(8,128)}, f32[6,4,32,128]{3,2,1,0:T(8,128)}, ...) custom-call(s32[2,3]{1,0:T(2,128)S(1)} %copy-done.11, ...), custom_call_target="tpu_custom_call" | custom-call | flops 20000000 | bytes 14725120 | tf_op jit(solution)/shard_map/last_finish/pallas_call | solution.py:453
  (29 shorter events, 0.1 us)
Async XLA Ops:
  0.6 17.3 %copy-start.1 = (f32[6,4,32,128]{3,2,1,0:T(8,128)S(1)}, f32[6,4,32,128]{3,2,1,0:T(8,128)}, u32[]{:S(2)}) copy-start(f32[6,4,32,128]{3,2,1,0:T(8,128)} %sc.1) | copy-start | bytes 1179652
  0.6 17.2 %copy-start.12 = (f32[8,5]{1,0:T(8,128)S(1)}, f32[8,5]{1,0:T(8,128)}, u32[]{:S(2)}) copy-start(f32[8,5]{1,0:T(8,128)} %param.23) | copy-start | bytes 484
  0.7 17.3 %copy-start.8 = (s32[4,32,128]{2,1,0:T(8,128)S(1)}, s32[4,32,128]{2,1,0:T(8,128)}, u32[]{:S(2)}) copy-start(s32[4,32,128]{2,1,0:T(8,128)} %rest_1_.2) | copy-start | bytes 196612
  0.7 17.3 %copy-start.7 = (f32[3,4,32,128]{3,2,1,0:T(8,128)S(1)}, f32[3,4,32,128]{3,2,1,0:T(8,128)}, u32[]{:S(2)}) copy-start(f32[3,4,32,128]{3,2,1,0:T(8,128)} %rest_5_.1) | copy-start | bytes 589828
  0.7 17.3 %copy-start.6 = (s32[12,16,384]{2,1,0:T(8,128)S(1)}, s32[12,16,384]{2,1,0:T(8,128)}, u32[]{:S(2)}) copy-start(s32[12,16,384]{2,1,0:T(8,128)} %rest_0_.2) | copy-start | bytes 884740
  3.8 21.6 %collective-permute-start.1 = (f32[8,128]{1,0:T(8,128)}, f32[8,128]{1,0:T(8,128)S(1)}, u32[]{:S(2)}, u32[]{:S(2)}) collective-permute-start(f32[8,128]{1,0:T(8,128)} %get-tuple-element.61), channel_id=1, source_target_pairs={{4,3},{8,7},{12,11},{16,15},{20,19},{24,23},{28,27},{32,31},{36,35... | collective-permute-start | bytes 12296 | tf_op jit(solution)/shard_map/ppermute | solution.py:688
  12.7 12.6 %collective-permute-start = (f32[72,384]{1,0:T(8,128)}, f32[72,384]{1,0:T(8,128)S(1)}, u32[]{:S(2)}, u32[]{:S(2)}) collective-permute-start(f32[72,384]{1,0:T(8,128)} %get-tuple-element.60), channel_id=1, source_target_pairs={{1,2},{3,0},{2,1},{0,3},{5,6},{7,4},{6,5},{4,7},{9,10},{11,8},{10,... | collective-permute-start | bytes 331784 | tf_op jit(solution)/shard_map/ppermute | solution.py:687
  12.8 12.5 %collective-permute-start.2 = (f32[72,384]{1,0:T(8,128)}, f32[72,384]{1,0:T(8,128)S(1)}, u32[]{:S(2)}, u32[]{:S(2)}) collective-permute-start(f32[72,384]{1,0:T(8,128)} %get-tuple-element.62), channel_id=1, source_target_pairs={{0,1},{2,3},{1,0},{3,2},{4,5},{6,7},{5,4},{7,6},{8,9},{10,11},{9,8... | collective-permute-start | bytes 331784 | tf_op jit(solution)/shard_map/ppermute | solution.py:689
  12.9 12.5 %collective-permute-start.3 = (f32[144,384]{1,0:T(8,128)}, f32[144,384]{1,0:T(8,128)S(1)}, u32[]{:S(2)}, u32[]{:S(2)}) collective-permute-start(f32[144,384]{1,0:T(8,128)} %get-tuple-element.63), channel_id=1, source_target_pairs={{4,8},{12,16},{20,24},{28,32},{36,40},{44,48},{52,56},{60,64},{68,... | collective-permute-start | bytes 663560 | tf_op jit(solution)/shard_map/ppermute | solution.py:690
  13.6 11.8 %collective-permute-start.4 = (f32[144,384]{1,0:T(8,128)}, f32[144,384]{1,0:T(8,128)S(1)}, u32[]{:S(2)}, u32[]{:S(2)}) collective-permute-start(f32[144,384]{1,0:T(8,128)} %get-tuple-element.64), channel_id=1, source_target_pairs={{0,4},{8,12},{16,20},{24,28},{32,36},{40,44},{48,52},{56,60},{64,6... | collective-permute-start | bytes 663560 | tf_op jit(solution)/shard_map/ppermute | solution.py:691
  18.0 1.5 %copy-start = (f32[6,12,16,384]{3,2,1,0:T(8,128)S(1)}, f32[6,12,16,384]{3,2,1,0:T(8,128)}, u32[]{:S(2)}) copy-start(f32[6,12,16,384]{3,2,1,0:T(8,128)} %sf.1) | copy-start | bytes 5308420
  19.5 1.2 %copy-start.3 = (f32[3,12,16,384]{3,2,1,0:T(8,128)S(1)}, f32[3,12,16,384]{3,2,1,0:T(8,128)}, u32[]{:S(2)}) copy-start(f32[3,12,16,384]{3,2,1,0:T(8,128)} %rest_4_.1) | copy-start | bytes 2654212
  20.6 4.8 %copy-start.10 = (s32[2,3]{1,0:T(2,128)S(1)}, s32[2,3]{1,0:T(2,128)}, u32[]{:S(2)}) copy-start(s32[2,3]{1,0:T(2,128)} %restrict.7) | copy-start | bytes 76
  20.6 4.8 %copy-start.11 = (s32[2,3]{1,0:T(2,128)S(1)}, s32[2,3]{1,0:T(2,128)}, u32[]{:S(2)}) copy-start(s32[2,3]{1,0:T(2,128)} %interp.7) | copy-start | bytes 76
  25.4 18.9 %copy-start.2 = (f32[6,12,16,384]{3,2,1,0:T(8,128)S(1)}, f32[6,12,16,384]{3,2,1,0:T(8,128)}, u32[]{:S(2)}) copy-start(f32[6,12,16,384]{3,2,1,0:T(8,128)} %mf.1) | copy-start | bytes 5308420
  25.4 18.9 %copy-start.4 = (f32[6,4,32,128]{3,2,1,0:T(8,128)S(1)}, f32[6,4,32,128]{3,2,1,0:T(8,128)}, u32[]{:S(2)}) copy-start(f32[6,4,32,128]{3,2,1,0:T(8,128)} %mc.1) | copy-start | bytes 1179652
  26.5 20.1 %collective-permute-start.8 = (f32[144,384]{1,0:T(8,128)S(1)}, f32[144,384]{1,0:T(8,128)S(1)}, u32[]{:S(2)}, u32[]{:S(2)}) collective-permute-start(f32[144,384]{1,0:T(8,128)S(1)} %get-tuple-element.72), channel_id=1, source_target_pairs={{4,8},{12,16},{20,24},{28,32},{36,40},{44,48},{52,56},{60,64},{68,... | collective-permute-start | bytes 663560 | tf_op jit(solution)/shard_map/ppermute | solution.py:690
  29.8 16.9 %collective-permute-start.9 = (f32[144,384]{1,0:T(8,128)S(1)}, f32[144,384]{1,0:T(8,128)S(1)}, u32[]{:S(2)}, u32[]{:S(2)}) collective-permute-start(f32[144,384]{1,0:T(8,128)S(1)} %get-tuple-element.73), channel_id=1, source_target_pairs={{0,4},{8,12},{16,20},{24,28},{32,36},{40,44},{48,52},{56,60},{64,6... | collective-permute-start | bytes 663560 | tf_op jit(solution)/shard_map/ppermute | solution.py:691
  29.8 16.8 %collective-permute-start.5 = (f32[72,384]{1,0:T(8,128)S(1)}, f32[72,384]{1,0:T(8,128)S(1)}, u32[]{:S(2)}, u32[]{:S(2)}) collective-permute-start(f32[72,384]{1,0:T(8,128)S(1)} %get-tuple-element.69), channel_id=1, source_target_pairs={{1,2},{3,0},{2,1},{0,3},{5,6},{7,4},{6,5},{4,7},{9,10},{11,8},{10,... | collective-permute-start | bytes 331784 | tf_op jit(solution)/shard_map/ppermute | solution.py:687
  35.2 11.4 %collective-permute-start.7 = (f32[72,384]{1,0:T(8,128)S(1)}, f32[72,384]{1,0:T(8,128)S(1)}, u32[]{:S(2)}, u32[]{:S(2)}) collective-permute-start(f32[72,384]{1,0:T(8,128)S(1)} %get-tuple-element.71), channel_id=1, source_target_pairs={{0,1},{2,3},{1,0},{3,2},{4,5},{6,7},{5,4},{7,6},{8,9},{10,11},{9,8... | collective-permute-start | bytes 331784 | tf_op jit(solution)/shard_map/ppermute | solution.py:689
  35.7 10.9 %collective-permute-start.6 = (f32[8,128]{1,0:T(8,128)S(1)}, f32[8,128]{1,0:T(8,128)S(1)}, u32[]{:S(2)}, u32[]{:S(2)}) collective-permute-start(f32[8,128]{1,0:T(8,128)S(1)} %get-tuple-element.70), channel_id=1, source_target_pairs={{4,3},{8,7},{12,11},{16,15},{20,19},{24,23},{28,27},{32,31},{36,35... | collective-permute-start | bytes 12296 | tf_op jit(solution)/shard_map/ppermute | solution.py:688
  46.6 15.9 %copy-start.5 = (f32[12,16,384]{2,1,0:T(8,128)S(1)}, f32[12,16,384]{2,1,0:T(8,128)}, u32[]{:S(2)}) copy-start(f32[12,16,384]{2,1,0:T(8,128)} %rest_0_.3) | copy-start | bytes 884740
  46.7 15.9 %copy-start.9 = (f32[4,32,128]{2,1,0:T(8,128)S(1)}, f32[4,32,128]{2,1,0:T(8,128)}, u32[]{:S(2)}) copy-start(f32[4,32,128]{2,1,0:T(8,128)} %rest_1_.3) | copy-start | bytes 196612
  48.1 19.8 %collective-permute-start.13 = (f32[144,384]{1,0:T(8,128)S(1)}, f32[144,384]{1,0:T(8,128)S(1)}, u32[]{:S(2)}, u32[]{:S(2)}) collective-permute-start(f32[144,384]{1,0:T(8,128)S(1)} %get-tuple-element.83), channel_id=1, source_target_pairs={{4,8},{12,16},{20,24},{28,32},{36,40},{44,48},{52,56},{60,64},{68,... | collective-permute-start | bytes 663560 | tf_op jit(solution)/shard_map/ppermute | solution.py:690
  49.8 18.1 %collective-permute-start.14 = (f32[144,384]{1,0:T(8,128)S(1)}, f32[144,384]{1,0:T(8,128)S(1)}, u32[]{:S(2)}, u32[]{:S(2)}) collective-permute-start(f32[144,384]{1,0:T(8,128)S(1)} %get-tuple-element.84), channel_id=1, source_target_pairs={{0,4},{8,12},{16,20},{24,28},{32,36},{40,44},{48,52},{56,60},{64,6... | collective-permute-start | bytes 663560 | tf_op jit(solution)/shard_map/ppermute | solution.py:691
  49.8 18.1 %collective-permute-start.10 = (f32[72,384]{1,0:T(8,128)S(1)}, f32[72,384]{1,0:T(8,128)S(1)}, u32[]{:S(2)}, u32[]{:S(2)}) collective-permute-start(f32[72,384]{1,0:T(8,128)S(1)} %get-tuple-element.80), channel_id=1, source_target_pairs={{1,2},{3,0},{2,1},{0,3},{5,6},{7,4},{6,5},{4,7},{9,10},{11,8},{10,... | collective-permute-start | bytes 331784 | tf_op jit(solution)/shard_map/ppermute | solution.py:687
  54.8 13.1 %collective-permute-start.12 = (f32[72,384]{1,0:T(8,128)S(1)}, f32[72,384]{1,0:T(8,128)S(1)}, u32[]{:S(2)}, u32[]{:S(2)}) collective-permute-start(f32[72,384]{1,0:T(8,128)S(1)} %get-tuple-element.82), channel_id=1, source_target_pairs={{0,1},{2,3},{1,0},{3,2},{4,5},{6,7},{5,4},{7,6},{8,9},{10,11},{9,8... | collective-permute-start | bytes 331784 | tf_op jit(solution)/shard_map/ppermute | solution.py:689
  54.9 13.0 %collective-permute-start.11 = (f32[8,128]{1,0:T(8,128)S(1)}, f32[8,128]{1,0:T(8,128)S(1)}, u32[]{:S(2)}, u32[]{:S(2)}) collective-permute-start(f32[8,128]{1,0:T(8,128)S(1)} %get-tuple-element.81), channel_id=1, source_target_pairs={{4,3},{8,7},{12,11},{16,15},{20,19},{24,23},{28,27},{32,31},{36,35... | collective-permute-start | bytes 12296 | tf_op jit(solution)/shard_map/ppermute | solution.py:688
  69.0 16.5 %collective-permute-start.18 = (f32[144,384]{1,0:T(8,128)S(1)}, f32[144,384]{1,0:T(8,128)S(1)}, u32[]{:S(2)}, u32[]{:S(2)}) collective-permute-start(f32[144,384]{1,0:T(8,128)S(1)} %get-tuple-element.92), channel_id=1, source_target_pairs={{4,8},{12,16},{20,24},{28,32},{36,40},{44,48},{52,56},{60,64},{68,... | collective-permute-start | bytes 663560 | tf_op jit(solution)/shard_map/ppermute | solution.py:690
  69.4 16.1 %collective-permute-start.19 = (f32[144,384]{1,0:T(8,128)S(1)}, f32[144,384]{1,0:T(8,128)S(1)}, u32[]{:S(2)}, u32[]{:S(2)}) collective-permute-start(f32[144,384]{1,0:T(8,128)S(1)} %get-tuple-element.93), channel_id=1, source_target_pairs={{0,4},{8,12},{16,20},{24,28},{32,36},{40,44},{48,52},{56,60},{64,6... | collective-permute-start | bytes 663560 | tf_op jit(solution)/shard_map/ppermute | solution.py:691
  69.7 15.8 %collective-permute-start.15 = (f32[72,384]{1,0:T(8,128)S(1)}, f32[72,384]{1,0:T(8,128)S(1)}, u32[]{:S(2)}, u32[]{:S(2)}) collective-permute-start(f32[72,384]{1,0:T(8,128)S(1)} %get-tuple-element.89), channel_id=1, source_target_pairs={{1,2},{3,0},{2,1},{0,3},{5,6},{7,4},{6,5},{4,7},{9,10},{11,8},{10,... | collective-permute-start | bytes 331784 | tf_op jit(solution)/shard_map/ppermute | solution.py:687
  72.5 13.0 %collective-permute-start.17 = (f32[72,384]{1,0:T(8,128)S(1)}, f32[72,384]{1,0:T(8,128)S(1)}, u32[]{:S(2)}, u32[]{:S(2)}) collective-permute-start(f32[72,384]{1,0:T(8,128)S(1)} %get-tuple-element.91), channel_id=1, source_target_pairs={{0,1},{2,3},{1,0},{3,2},{4,5},{6,7},{5,4},{7,6},{8,9},{10,11},{9,8... | collective-permute-start | bytes 331784 | tf_op jit(solution)/shard_map/ppermute | solution.py:689
  72.5 13.0 %collective-permute-start.16 = (f32[8,128]{1,0:T(8,128)S(1)}, f32[8,128]{1,0:T(8,128)S(1)}, u32[]{:S(2)}, u32[]{:S(2)}) collective-permute-start(f32[8,128]{1,0:T(8,128)S(1)} %get-tuple-element.90), channel_id=1, source_target_pairs={{4,3},{8,7},{12,11},{16,15},{20,19},{24,23},{28,27},{32,31},{36,35... | collective-permute-start | bytes 12296 | tf_op jit(solution)/shard_map/ppermute | solution.py:688

commit v2 on v1

--- a/solution.py
+++ b/solution.py
@@ -423,7 +423,7 @@
 VMEM = pl.BlockSpec(memory_space=pltpu.VMEM)
 HBM = pl.BlockSpec(memory_space=pltpu.HBM)
 LIMIT = 24 * 1024 * 1024
-PACK_LIMIT = 63 * 1024 * 1024
+PACK_LIMIT = 62 * 1024 * 1024
 FIRST_LIMIT = 40 * 1024 * 1024
 
 
@@ -497,11 +497,21 @@
 def material_rows(table, zone, out):
     def step(x, carry):
         kind = zone[x]
-        for column in range(7):
-            value = jnp.full(kind.shape, table[7, column])
+
+        def column(index):
+            value = jnp.full(kind.shape, table[7, index])
             for level in range(7):
-                value = jnp.where(kind == level, table[level, column], value)
-            out[column, x] = value
+                value = jnp.where(kind == level, table[level, index], value)
+            return value
+
+        lame, shear, decay = column(1), column(2), column(3)
+        out[CB, x] = column(0)
+        out[LAME, x] = lame
+        out[MU2, x] = 2.0 * shear
+        out[DECAY, x] = decay
+        out[DAMP, x] = column(4) * (1.0 - decay)
+        out[ISO, x] = lame / (3.0 * lame + 2.0 * shear)
+        out[SCALE, x] = 0.5 / shear
         return carry
 
     lax.fori_loop(0, zone.shape[0], step, 0)
@@ -708,19 +718,6 @@
     restrict_weight,
 ):
     sizes = Sizes(stress_fine.shape[1:], stress_coarse.shape[1:])
-    buoyancy, lame, shear, decay, damping = [zone_table[:, i] for i in range(5)]
-    table = jnp.stack(
-        [
-            buoyancy,
-            lame,
-            2.0 * shear,
-            decay,
-            damping * (1.0 - decay),
-            lame / (3.0 * lame + 2.0 * shear),
-            0.5 / shear,
-        ],
-        axis=1,
-    )
     velocity = (velocity_fine, velocity_coarse)
     stress = (stress_fine, stress_coarse)
     memory = (memory_fine, memory_coarse)
@@ -729,7 +726,7 @@
     for step in range(STEPS):
         halos = exchanged(outgoing)
         if step == 0:
-            velocity, props = first_bulk(table, (zone_fine, zone_coarse), stress, velocity)
+            velocity, props = first_bulk(zone_table, (zone_fine, zone_coarse), stress, velocity)
         else:
             velocity, peak = velocity_bulk(stress, props, velocity, peak)
         velocity, outgoing = velocity_finish(

time: 92 us -> 85.4 us (0.928)
  starting transfers between devices: 60.5 us -> 53.7 us
  local copies, waits for them, and re-layouts: 2.77 us -> 3.85 us
    ppermute x4, starting transfers between devices: 36 us -> 29.8 us  [exchanged(): diag = lax.ppermute(diag, ('lat', 'depth'), across)]
    ppermute x4, starting transfers between devices: 5.95 us -> 2.4 us  [exchanged(): latO = lax.ppermute(latO, 'lat', swaps(lat, 1))]
    ppermute x4, starting transfers between devices: 4.54 us -> 6.47 us  [exchanged(): latE = lax.ppermute(latE, 'lat', swaps(lat, 0))]
    unnamed x26, local copies, waits for them, and re-layouts: 2.69 us -> 3.85 us
  transfers between devices with their start and end apart: 20 -> 20, of which waited for: 0 -> 0; matrix products, arithmetic and copies ran while one was open for 0% -> 0% of each run, Pallas kernels for 16% -> 17%
where the time goes in v2:
time: 85.4 us; the launch traced here: 85.1 us
  starting transfers between devices  53.7 us (63%)
  Pallas kernels  26.4 us (31%)
  local copies, waits for them, and re-layouts  3.85 us (5%)
  between operations  1.21 us (1%)
    ppermute x4, starting transfers between devices, exchanged(): diag = lax.ppermute(diag, ('lat', 'depth'), across)  29.8 us
    pallas_call x9, Pallas kernels, call(): pl.pallas_call(kernel, name=name, out_shape=outs, in_specs=[SMEM] * len(s...  26.4 us
    ppermute x4, starting transfers between devices, exchanged(): depO = lax.ppermute(depO, 'depth', swaps(depth, 1))  14.2 us
    ppermute x4, starting transfers between devices, exchanged(): latE = lax.ppermute(latE, 'lat', swaps(lat, 0))  6.47 us
    unnamed x26, local copies, waits for them, and re-layouts  3.85 us
    ppermute x4, starting transfers between devices, exchanged(): latO = lax.ppermute(latO, 'lat', swaps(lat, 1))  2.4 us
  transfers between devices with their start and end apart: 20, of which 0 were waited for; matrix products, arithmetic and copies ran while one was open for 0% of the time, Pallas kernels for 17%

profile of v2, /device:TPU:4, one launch (start us, length us, event | category | flops | bytes accessed | tf_op | source)
XLA Modules:
  0.0 85.1 jit_solution(13006189406801786511)
XLA Ops:
  0.7 3.1 %pack_stress.1 = (f32[72,384]{1,0:T(8,128)}, f32[8,128]{1,0:T(8,128)}, f32[72,384]{1,0:T(8,128)}, f32[144,384]{1,0:T(8,128)}, f32[144,384]{1,0:T(8,128)}) custom-call(s32[2,3]{1,0:T(2,128)} %restrict.7, f32[6,12,16,384]{3,2,1,0:T(8,128)} %sf.1, f32[6,4,32,128]{3,2,1,0:T(8,128)} %sc.1), custom_call_target="tpu_custom_call" | custom-call | flops 1000000 | bytes 2830336 | tf_op jit(solution)/shard_map/pack_stress/pallas_call | solution.py:453
  3.7 0.6 collective-permute-start.3
  4.4 2.2 %collective-permute-start.4 = (f32[144,384]{1,0:T(8,128)}, f32[144,384]{1,0:T(8,128)S(1)}, u32[]{:S(2)}, u32[]{:S(2)}) collective-permute-start(f32[144,384]{1,0:T(8,128)} %get-tuple-element.64), channel_id=1, source_target_pairs={{0,4},{8,12},{16,20},{24,28},{32,36},{40,44},{48,52},{56,60},{64,6... | collective-permute-start | bytes 663560 | tf_op jit(solution)/shard_map/ppermute | solution.py:701
  6.5 6.5 %collective-permute-start = (f32[72,384]{1,0:T(8,128)}, f32[72,384]{1,0:T(8,128)S(1)}, u32[]{:S(2)}, u32[]{:S(2)}) collective-permute-start(f32[72,384]{1,0:T(8,128)} %get-tuple-element.60), channel_id=1, source_target_pairs={{1,2},{3,0},{2,1},{0,3},{5,6},{7,4},{6,5},{4,7},{9,10},{11,8},{10,... | collective-permute-start | bytes 331784 | tf_op jit(solution)/shard_map/ppermute | solution.py:697
  13.0 0.8 collective-permute-start.2
  13.8 7.3 %collective-permute-start.1 = (f32[8,128]{1,0:T(8,128)}, f32[8,128]{1,0:T(8,128)S(1)}, u32[]{:S(2)}, u32[]{:S(2)}) collective-permute-start(f32[8,128]{1,0:T(8,128)} %get-tuple-element.61), channel_id=1, source_target_pairs={{4,3},{8,7},{12,11},{16,15},{20,19},{24,23},{28,27},{32,31},{36,35... | collective-permute-start | bytes 12296 | tf_op jit(solution)/shard_map/ppermute | solution.py:698
  21.2 0.0 copy-start.1
  21.2 1.0 %copy-done.1 = f32[6,4,32,128]{3,2,1,0:T(8,128)S(1)} copy-done((f32[6,4,32,128]{3,2,1,0:T(8,128)S(1)}, f32[6,4,32,128]{3,2,1,0:T(8,128)}, u32[]{:S(2)}) %copy-start.1) | copy-done | bytes 393240
  22.2 1.2 %copy-done.3 = f32[3,12,16,384]{3,2,1,0:T(8,128)S(1)} copy-done((f32[3,12,16,384]{3,2,1,0:T(8,128)S(1)}, f32[3,12,16,384]{3,2,1,0:T(8,128)}, u32[]{:S(2)}) %copy-start.3) | copy-done | bytes 884760
  23.4 1.0 %copy-done.6 = s32[12,16,384]{2,1,0:T(8,128)S(1)} copy-done((s32[12,16,384]{2,1,0:T(8,128)S(1)}, s32[12,16,384]{2,1,0:T(8,128)}, u32[]{:S(2)}) %copy-start.6) | copy-done | bytes 294936
  24.3 0.7 copy-done.12
  25.0 4.5 %first_bulk.1 = (f32[3,12,16,384]{3,2,1,0:T(8,128)S(1)}, f32[3,4,32,128]{3,2,1,0:T(8,128)S(1)}, f32[7,12,16,384]{3,2,1,0:T(8,128)S(1)}, f32[7,4,32,128]{3,2,1,0:T(8,128)S(1)}) custom-call(f32[8,5]{1,0:T(8,128)S(1)} %copy-done.12, s32[12,16,384]{2,1,0:T(8,128)S(1)} %copy-done.6, s32[4,32,128]{2,1,0:T(8,128)S(1)} %copy-done.8, f32[6,12,16,384]{3,2,1,0:T(8,128)S(1)} %copy-done, ...), custom_call_target="tpu_custom_call" | custom-call | flops 2000000 | bytes 7208960 | tf_op jit(solution)/shard_map/first_bulk/pallas_call | solution.py:453
  29.5 0.0 collective-permute-done.1.rest_1_
  29.5 0.0 collective-permute-done.rest_0_
  29.5 0.0 collective-permute-done.3.rest_3_
  29.5 0.0 collective-permute-done.4.rest_4_
  29.6 0.0 copy-start.2
  29.6 0.0 copy-start.4
  29.6 1.1 %velocity_finish.2 = (f32[3,12,16,384]{3,2,1,0:T(8,128)S(1)}, f32[3,4,32,128]{3,2,1,0:T(8,128)S(1)}, f32[72,384]{1,0:T(8,128)S(1)}, f32[8,128]{1,0:T(8,128)S(1)}...) custom-call(s32[2,3]{1,0:T(2,128)S(1)} %copy-done.11, s32[2,3]{1,0:T(2,128)S(1)} %copy-done.10, ...), custom_call_target="tpu_custom_call" | custom-call | flops 10000000 | bytes 6021120 | tf_op jit(solution)/shard_map/velocity_finish/pallas_call | solution.py:453
  30.7 0.1 collective-permute-start.8
  30.8 0.1 collective-permute-start.9
  30.9 0.6 collective-permute-start.5
  31.5 0.0 collective-permute-start.7
  31.5 8.8 %collective-permute-start.6 = (f32[8,128]{1,0:T(8,128)S(1)}, f32[8,128]{1,0:T(8,128)S(1)}, u32[]{:S(2)}, u32[]{:S(2)}) collective-permute-start(f32[8,128]{1,0:T(8,128)S(1)} %get-tuple-element.70), channel_id=1, source_target_pairs={{4,3},{8,7},{12,11},{16,15},{20,19},{24,23},{28,27},{32,31},{36,35... | collective-permute-start | bytes 12296 | tf_op jit(solution)/shard_map/ppermute | solution.py:698
  40.3 2.2 %stress_bulk.2 = (f32[6,12,16,384]{3,2,1,0:T(8,128)S(1)}, f32[6,4,32,128]{3,2,1,0:T(8,128)S(1)}, f32[6,12,16,384]{3,2,1,0:T(8,128)S(1)}, f32[6,4,32,128]{3,2,1,0:T(8,128)S(1)}) custom-call(f32[3,12,16,384]{3,2,1,0:T(8,128)S(1)} %get-tuple-element.74.vf, f32[3,4,32,128]{3,2,1,0:T(8,128)S(1)} %get-tuple-element.75.vc, ...), custom_call_target="tpu_custom_call" | custom-call | flops 2000000 | bytes 12255232 | tf_op jit(solution)/shard_map/stress_bulk/pallas_call | solution.py:453
  42.6 0.0 collective-permute-done.6.rest_1_
  42.6 0.0 collective-permute-done.7.rest_2_
  42.6 0.0 collective-permute-done.8.rest_3_
  42.6 0.0 copy-start.5
  42.6 0.0 copy-start.9
  42.6 1.4 %stress_finish.1 = (f32[6,12,16,384]{3,2,1,0:T(8,128)S(1)}, f32[6,4,32,128]{3,2,1,0:T(8,128)S(1)}, f32[6,12,16,384]{3,2,1,0:T(8,128)S(1)}, f32[6,4,32,128]{3,2,1...) custom-call(s32[2,3]{1,0:T(2,128)S(1)} %copy-done.11, ...), custom_call_target="tpu_custom_call" | custom-call | flops 20000000 | bytes 12509184 | tf_op jit(solution)/shard_map/stress_finish/pallas_call | solution.py:453
  44.1 1.6 %collective-permute-start.13 = (f32[144,384]{1,0:T(8,128)S(1)}, f32[144,384]{1,0:T(8,128)S(1)}, u32[]{:S(2)}, u32[]{:S(2)}) collective-permute-start(f32[144,384]{1,0:T(8,128)S(1)} %get-tuple-element.83), channel_id=1, source_target_pairs={{4,8},{12,16},{20,24},{28,32},{36,40},{44,48},{52,56},{60,64},{68,... | collective-permute-start | bytes 663560 | tf_op jit(solution)/shard_map/ppermute | solution.py:700
  45.6 2.2 %collective-permute-start.14 = (f32[144,384]{1,0:T(8,128)S(1)}, f32[144,384]{1,0:T(8,128)S(1)}, u32[]{:S(2)}, u32[]{:S(2)}) collective-permute-start(f32[144,384]{1,0:T(8,128)S(1)} %get-tuple-element.84), channel_id=1, source_target_pairs={{0,4},{8,12},{16,20},{24,28},{32,36},{40,44},{48,52},{56,60},{64,6... | collective-permute-start | bytes 663560 | tf_op jit(solution)/shard_map/ppermute | solution.py:701
  47.9 4.8 %collective-permute-start.10 = (f32[72,384]{1,0:T(8,128)S(1)}, f32[72,384]{1,0:T(8,128)S(1)}, u32[]{:S(2)}, u32[]{:S(2)}) collective-permute-start(f32[72,384]{1,0:T(8,128)S(1)} %get-tuple-element.80), channel_id=1, source_target_pairs={{1,2},{3,0},{2,1},{0,3},{5,6},{7,4},{6,5},{4,7},{9,10},{11,8},{10,... | collective-permute-start | bytes 331784 | tf_op jit(solution)/shard_map/ppermute | solution.py:697
  52.7 4.4 %collective-permute-start.11 = (f32[8,128]{1,0:T(8,128)S(1)}, f32[8,128]{1,0:T(8,128)S(1)}, u32[]{:S(2)}, u32[]{:S(2)}) collective-permute-start(f32[8,128]{1,0:T(8,128)S(1)} %get-tuple-element.81), channel_id=1, source_target_pairs={{4,3},{8,7},{12,11},{16,15},{20,19},{24,23},{28,27},{32,31},{36,35... | collective-permute-start | bytes 12296 | tf_op jit(solution)/shard_map/ppermute | solution.py:698
  57.2 5.3 %velocity_bulk.1 = (f32[3,12,16,384]{3,2,1,0:T(8,128)S(1)}, f32[3,4,32,128]{3,2,1,0:T(8,128)S(1)}, f32[12,16,384]{2,1,0:T(8,128)S(1)}, f32[4,32,128]{2,1,0:T(8,128)S(1)}) custom-call(f32[6,12,16,384]{3,2,1,0:T(8,128)S(1)} %get-tuple-element.85.sf, f32[6,4,32,128]{3,2,1,0:T(8,128)S(1)} %get-tuple-element.86.sc, ...), custom_call_target="tpu_custom_call" | custom-call | flops 2000000 | bytes 7569408 | tf_op jit(solution)/shard_map/velocity_bulk/pallas_call | solution.py:453
  62.4 0.0 collective-permute-done.11.rest_1_
  62.4 0.0 collective-permute-done.10.rest_0_
  62.5 0.0 collective-permute-done.13.rest_3_
  62.5 0.0 collective-permute-done.14.rest_4_
  62.5 1.1 %velocity_finish.3 = (f32[3,12,16,384]{3,2,1,0:T(8,128)S(1)}, f32[3,4,32,128]{3,2,1,0:T(8,128)S(1)}, f32[72,384]{1,0:T(8,128)S(1)}, f32[8,128]{1,0:T(8,128)S(1)}...) custom-call(s32[2,3]{1,0:T(2,128)S(1)} %copy-done.11, s32[2,3]{1,0:T(2,128)S(1)} %copy-done.10, ...), custom_call_target="tpu_custom_call" | custom-call | flops 10000000 | bytes 6021120 | tf_op jit(solution)/shard_map/velocity_finish/pallas_call | solution.py:453
  63.6 0.1 collective-permute-start.18
  63.7 2.0 %collective-permute-start.19 = (f32[144,384]{1,0:T(8,128)S(1)}, f32[144,384]{1,0:T(8,128)S(1)}, u32[]{:S(2)}, u32[]{:S(2)}) collective-permute-start(f32[144,384]{1,0:T(8,128)S(1)} %get-tuple-element.93), channel_id=1, source_target_pairs={{0,4},{8,12},{16,20},{24,28},{32,36},{40,44},{48,52},{56,60},{64,6... | collective-permute-start | bytes 663560 | tf_op jit(solution)/shard_map/ppermute | solution.py:701
  65.7 2.2 %collective-permute-start.15 = (f32[72,384]{1,0:T(8,128)S(1)}, f32[72,384]{1,0:T(8,128)S(1)}, u32[]{:S(2)}, u32[]{:S(2)}) collective-permute-start(f32[72,384]{1,0:T(8,128)S(1)} %get-tuple-element.89), channel_id=1, source_target_pairs={{1,2},{3,0},{2,1},{0,3},{5,6},{7,4},{6,5},{4,7},{9,10},{11,8},{10,... | collective-permute-start | bytes 331784 | tf_op jit(solution)/shard_map/ppermute | solution.py:697
  67.9 0.0 collective-permute-start.17
  67.9 9.2 %collective-permute-start.16 = (f32[8,128]{1,0:T(8,128)S(1)}, f32[8,128]{1,0:T(8,128)S(1)}, u32[]{:S(2)}, u32[]{:S(2)}) collective-permute-start(f32[8,128]{1,0:T(8,128)S(1)} %get-tuple-element.90), channel_id=1, source_target_pairs={{4,3},{8,7},{12,11},{16,15},{20,19},{24,23},{28,27},{32,31},{36,35... | collective-permute-start | bytes 12296 | tf_op jit(solution)/shard_map/ppermute | solution.py:698
  77.2 2.2 %stress_bulk.3 = (f32[6,12,16,384]{3,2,1,0:T(8,128)S(1)}, f32[6,4,32,128]{3,2,1,0:T(8,128)S(1)}, f32[6,12,16,384]{3,2,1,0:T(8,128)S(1)}, f32[6,4,32,128]{3,2,1,0:T(8,128)S(1)}) custom-call(f32[3,12,16,384]{3,2,1,0:T(8,128)S(1)} %get-tuple-element.94.vf.rest_13_, f32[3,4,32,128]{3,2,1,0:T(8,128)S(1)} %get-tuple-element.95.vc.rest_14_, ...), custom_call_target="tpu_custom_call" | custom-call | flops 2000000 | bytes 12255232 | tf_op jit(solution)/shard_map/stress_bulk/pallas_call | solution.py:453
  79.5 5.5 %last_finish.1 = (f32[3,12,16,384]{3,2,1,0:T(8,128)}, f32[3,4,32,128]{3,2,1,0:T(8,128)}, f32[6,12,16,384]{3,2,1,0:T(8,128)}, f32[6,4,32,128]{3,2,1,0:T(8,128)}, ...) custom-call(s32[2,3]{1,0:T(2,128)S(1)} %copy-done.11, ...), custom_call_target="tpu_custom_call" | custom-call | flops 20000000 | bytes 14725120 | tf_op jit(solution)/shard_map/last_finish/pallas_call | solution.py:453
  (27 shorter events, 0.1 us)
Async XLA Ops:
  0.6 20.5 %copy-start = (f32[6,12,16,384]{3,2,1,0:T(8,128)S(1)}, f32[6,12,16,384]{3,2,1,0:T(8,128)}, u32[]{:S(2)}) copy-start(f32[6,12,16,384]{3,2,1,0:T(8,128)} %sf.1) | copy-start | bytes 5308420
  0.6 20.5 %copy-start.8 = (s32[4,32,128]{2,1,0:T(8,128)S(1)}, s32[4,32,128]{2,1,0:T(8,128)}, u32[]{:S(2)}) copy-start(s32[4,32,128]{2,1,0:T(8,128)} %rest_1_.2) | copy-start | bytes 196612
  0.7 20.5 %copy-start.7 = (f32[3,4,32,128]{3,2,1,0:T(8,128)S(1)}, f32[3,4,32,128]{3,2,1,0:T(8,128)}, u32[]{:S(2)}) copy-start(f32[3,4,32,128]{3,2,1,0:T(8,128)} %rest_5_.1) | copy-start | bytes 589828
  3.7 25.8 %collective-permute-start.3 = (f32[144,384]{1,0:T(8,128)}, f32[144,384]{1,0:T(8,128)S(1)}, u32[]{:S(2)}, u32[]{:S(2)}) collective-permute-start(f32[144,384]{1,0:T(8,128)} %get-tuple-element.63), channel_id=1, source_target_pairs={{4,8},{12,16},{20,24},{28,32},{36,40},{44,48},{52,56},{60,64},{68,... | collective-permute-start | bytes 663560 | tf_op jit(solution)/shard_map/ppermute | solution.py:700
  4.4 25.2 %collective-permute-start.4 = (f32[144,384]{1,0:T(8,128)}, f32[144,384]{1,0:T(8,128)S(1)}, u32[]{:S(2)}, u32[]{:S(2)}) collective-permute-start(f32[144,384]{1,0:T(8,128)} %get-tuple-element.64), channel_id=1, source_target_pairs={{0,4},{8,12},{16,20},{24,28},{32,36},{40,44},{48,52},{56,60},{64,6... | collective-permute-start | bytes 663560 | tf_op jit(solution)/shard_map/ppermute | solution.py:701
  6.5 23.0 %collective-permute-start = (f32[72,384]{1,0:T(8,128)}, f32[72,384]{1,0:T(8,128)S(1)}, u32[]{:S(2)}, u32[]{:S(2)}) collective-permute-start(f32[72,384]{1,0:T(8,128)} %get-tuple-element.60), channel_id=1, source_target_pairs={{1,2},{3,0},{2,1},{0,3},{5,6},{7,4},{6,5},{4,7},{9,10},{11,8},{10,... | collective-permute-start | bytes 331784 | tf_op jit(solution)/shard_map/ppermute | solution.py:697
  13.0 16.5 %collective-permute-start.2 = (f32[72,384]{1,0:T(8,128)}, f32[72,384]{1,0:T(8,128)S(1)}, u32[]{:S(2)}, u32[]{:S(2)}) collective-permute-start(f32[72,384]{1,0:T(8,128)} %get-tuple-element.62), channel_id=1, source_target_pairs={{0,1},{2,3},{1,0},{3,2},{4,5},{6,7},{5,4},{7,6},{8,9},{10,11},{9,8... | collective-permute-start | bytes 331784 | tf_op jit(solution)/shard_map/ppermute | solution.py:699
  13.8 15.7 %collective-permute-start.1 = (f32[8,128]{1,0:T(8,128)}, f32[8,128]{1,0:T(8,128)S(1)}, u32[]{:S(2)}, u32[]{:S(2)}) collective-permute-start(f32[8,128]{1,0:T(8,128)} %get-tuple-element.61), channel_id=1, source_target_pairs={{4,3},{8,7},{12,11},{16,15},{20,19},{24,23},{28,27},{32,31},{36,35... | collective-permute-start | bytes 12296 | tf_op jit(solution)/shard_map/ppermute | solution.py:698
  21.2 1.0 %copy-start.1 = (f32[6,4,32,128]{3,2,1,0:T(8,128)S(1)}, f32[6,4,32,128]{3,2,1,0:T(8,128)}, u32[]{:S(2)}) copy-start(f32[6,4,32,128]{3,2,1,0:T(8,128)} %sc.1) | copy-start | bytes 1179652
  22.2 1.2 %copy-start.3 = (f32[3,12,16,384]{3,2,1,0:T(8,128)S(1)}, f32[3,12,16,384]{3,2,1,0:T(8,128)}, u32[]{:S(2)}) copy-start(f32[3,12,16,384]{3,2,1,0:T(8,128)} %rest_4_.1) | copy-start | bytes 2654212
  23.4 1.0 %copy-start.6 = (s32[12,16,384]{2,1,0:T(8,128)S(1)}, s32[12,16,384]{2,1,0:T(8,128)}, u32[]{:S(2)}) copy-start(s32[12,16,384]{2,1,0:T(8,128)} %rest_0_.2) | copy-start | bytes 884740
  24.3 0.7 copy-start.12
  25.0 4.5 %copy-start.10 = (s32[2,3]{1,0:T(2,128)S(1)}, s32[2,3]{1,0:T(2,128)}, u32[]{:S(2)}) copy-start(s32[2,3]{1,0:T(2,128)} %restrict.7) | copy-start | bytes 76
  25.0 4.6 %copy-start.11 = (s32[2,3]{1,0:T(2,128)S(1)}, s32[2,3]{1,0:T(2,128)}, u32[]{:S(2)}) copy-start(s32[2,3]{1,0:T(2,128)} %interp.7) | copy-start | bytes 76
  29.6 10.8 %copy-start.2 = (f32[6,12,16,384]{3,2,1,0:T(8,128)S(1)}, f32[6,12,16,384]{3,2,1,0:T(8,128)}, u32[]{:S(2)}) copy-start(f32[6,12,16,384]{3,2,1,0:T(8,128)} %mf.1) | copy-start | bytes 5308420
  29.6 10.8 %copy-start.4 = (f32[6,4,32,128]{3,2,1,0:T(8,128)S(1)}, f32[6,4,32,128]{3,2,1,0:T(8,128)}, u32[]{:S(2)}) copy-start(f32[6,4,32,128]{3,2,1,0:T(8,128)} %mc.1) | copy-start | bytes 1179652
  30.7 11.9 %collective-permute-start.8 = (f32[144,384]{1,0:T(8,128)S(1)}, f32[144,384]{1,0:T(8,128)S(1)}, u32[]{:S(2)}, u32[]{:S(2)}) collective-permute-start(f32[144,384]{1,0:T(8,128)S(1)} %get-tuple-element.72), channel_id=1, source_target_pairs={{4,8},{12,16},{20,24},{28,32},{36,40},{44,48},{52,56},{60,64},{68,... | collective-permute-start | bytes 663560 | tf_op jit(solution)/shard_map/ppermute | solution.py:700
  30.8 11.8 %collective-permute-start.9 = (f32[144,384]{1,0:T(8,128)S(1)}, f32[144,384]{1,0:T(8,128)S(1)}, u32[]{:S(2)}, u32[]{:S(2)}) collective-permute-start(f32[144,384]{1,0:T(8,128)S(1)} %get-tuple-element.73), channel_id=1, source_target_pairs={{0,4},{8,12},{16,20},{24,28},{32,36},{40,44},{48,52},{56,60},{64,6... | collective-permute-start | bytes 663560 | tf_op jit(solution)/shard_map/ppermute | solution.py:701
  30.9 11.7 %collective-permute-start.5 = (f32[72,384]{1,0:T(8,128)S(1)}, f32[72,384]{1,0:T(8,128)S(1)}, u32[]{:S(2)}, u32[]{:S(2)}) collective-permute-start(f32[72,384]{1,0:T(8,128)S(1)} %get-tuple-element.69), channel_id=1, source_target_pairs={{1,2},{3,0},{2,1},{0,3},{5,6},{7,4},{6,5},{4,7},{9,10},{11,8},{10,... | collective-permute-start | bytes 331784 | tf_op jit(solution)/shard_map/ppermute | solution.py:697
  31.5 11.1 %collective-permute-start.7 = (f32[72,384]{1,0:T(8,128)S(1)}, f32[72,384]{1,0:T(8,128)S(1)}, u32[]{:S(2)}, u32[]{:S(2)}) collective-permute-start(f32[72,384]{1,0:T(8,128)S(1)} %get-tuple-element.71), channel_id=1, source_target_pairs={{0,1},{2,3},{1,0},{3,2},{4,5},{6,7},{5,4},{7,6},{8,9},{10,11},{9,8... | collective-permute-start | bytes 331784 | tf_op jit(solution)/shard_map/ppermute | solution.py:699
  31.5 11.0 %collective-permute-start.6 = (f32[8,128]{1,0:T(8,128)S(1)}, f32[8,128]{1,0:T(8,128)S(1)}, u32[]{:S(2)}, u32[]{:S(2)}) collective-permute-start(f32[8,128]{1,0:T(8,128)S(1)} %get-tuple-element.70), channel_id=1, source_target_pairs={{4,3},{8,7},{12,11},{16,15},{20,19},{24,23},{28,27},{32,31},{36,35... | collective-permute-start | bytes 12296 | tf_op jit(solution)/shard_map/ppermute | solution.py:698
  42.6 14.5 %copy-start.5 = (f32[12,16,384]{2,1,0:T(8,128)S(1)}, f32[12,16,384]{2,1,0:T(8,128)}, u32[]{:S(2)}) copy-start(f32[12,16,384]{2,1,0:T(8,128)} %rest_0_.3) | copy-start | bytes 884740
  42.6 14.5 %copy-start.9 = (f32[4,32,128]{2,1,0:T(8,128)S(1)}, f32[4,32,128]{2,1,0:T(8,128)}, u32[]{:S(2)}) copy-start(f32[4,32,128]{2,1,0:T(8,128)} %rest_1_.3) | copy-start | bytes 196612
  44.1 18.4 %collective-permute-start.13 = (f32[144,384]{1,0:T(8,128)S(1)}, f32[144,384]{1,0:T(8,128)S(1)}, u32[]{:S(2)}, u32[]{:S(2)}) collective-permute-start(f32[144,384]{1,0:T(8,128)S(1)} %get-tuple-element.83), channel_id=1, source_target_pairs={{4,8},{12,16},{20,24},{28,32},{36,40},{44,48},{52,56},{60,64},{68,... | collective-permute-start | bytes 663560 | tf_op jit(solution)/shard_map/ppermute | solution.py:700
  45.6 16.8 %collective-permute-start.14 = (f32[144,384]{1,0:T(8,128)S(1)}, f32[144,384]{1,0:T(8,128)S(1)}, u32[]{:S(2)}, u32[]{:S(2)}) collective-permute-start(f32[144,384]{1,0:T(8,128)S(1)} %get-tuple-element.84), channel_id=1, source_target_pairs={{0,4},{8,12},{16,20},{24,28},{32,36},{40,44},{48,52},{56,60},{64,6... | collective-permute-start | bytes 663560 | tf_op jit(solution)/shard_map/ppermute | solution.py:701
  47.9 14.6 %collective-permute-start.10 = (f32[72,384]{1,0:T(8,128)S(1)}, f32[72,384]{1,0:T(8,128)S(1)}, u32[]{:S(2)}, u32[]{:S(2)}) collective-permute-start(f32[72,384]{1,0:T(8,128)S(1)} %get-tuple-element.80), channel_id=1, source_target_pairs={{1,2},{3,0},{2,1},{0,3},{5,6},{7,4},{6,5},{4,7},{9,10},{11,8},{10,... | collective-permute-start | bytes 331784 | tf_op jit(solution)/shard_map/ppermute | solution.py:697
  52.7 9.8 %collective-permute-start.12 = (f32[72,384]{1,0:T(8,128)S(1)}, f32[72,384]{1,0:T(8,128)S(1)}, u32[]{:S(2)}, u32[]{:S(2)}) collective-permute-start(f32[72,384]{1,0:T(8,128)S(1)} %get-tuple-element.82), channel_id=1, source_target_pairs={{0,1},{2,3},{1,0},{3,2},{4,5},{6,7},{5,4},{7,6},{8,9},{10,11},{9,8... | collective-permute-start | bytes 331784 | tf_op jit(solution)/shard_map/ppermute | solution.py:699
  52.7 9.7 %collective-permute-start.11 = (f32[8,128]{1,0:T(8,128)S(1)}, f32[8,128]{1,0:T(8,128)S(1)}, u32[]{:S(2)}, u32[]{:S(2)}) collective-permute-start(f32[8,128]{1,0:T(8,128)S(1)} %get-tuple-element.81), channel_id=1, source_target_pairs={{4,3},{8,7},{12,11},{16,15},{20,19},{24,23},{28,27},{32,31},{36,35... | collective-permute-start | bytes 12296 | tf_op jit(solution)/shard_map/ppermute | solution.py:698
  63.6 15.9 %collective-permute-start.18 = (f32[144,384]{1,0:T(8,128)S(1)}, f32[144,384]{1,0:T(8,128)S(1)}, u32[]{:S(2)}, u32[]{:S(2)}) collective-permute-start(f32[144,384]{1,0:T(8,128)S(1)} %get-tuple-element.92), channel_id=1, source_target_pairs={{4,8},{12,16},{20,24},{28,32},{36,40},{44,48},{52,56},{60,64},{68,... | collective-permute-start | bytes 663560 | tf_op jit(solution)/shard_map/ppermute | solution.py:700
  63.7 15.8 %collective-permute-start.19 = (f32[144,384]{1,0:T(8,128)S(1)}, f32[144,384]{1,0:T(8,128)S(1)}, u32[]{:S(2)}, u32[]{:S(2)}) collective-permute-start(f32[144,384]{1,0:T(8,128)S(1)} %get-tuple-element.93), channel_id=1, source_target_pairs={{0,4},{8,12},{16,20},{24,28},{32,36},{40,44},{48,52},{56,60},{64,6... | collective-permute-start | bytes 663560 | tf_op jit(solution)/shard_map/ppermute | solution.py:701
  65.7 13.7 %collective-permute-start.15 = (f32[72,384]{1,0:T(8,128)S(1)}, f32[72,384]{1,0:T(8,128)S(1)}, u32[]{:S(2)}, u32[]{:S(2)}) collective-permute-start(f32[72,384]{1,0:T(8,128)S(1)} %get-tuple-element.89), channel_id=1, source_target_pairs={{1,2},{3,0},{2,1},{0,3},{5,6},{7,4},{6,5},{4,7},{9,10},{11,8},{10,... | collective-permute-start | bytes 331784 | tf_op jit(solution)/shard_map/ppermute | solution.py:697
  67.9 11.5 %collective-permute-start.17 = (f32[72,384]{1,0:T(8,128)S(1)}, f32[72,384]{1,0:T(8,128)S(1)}, u32[]{:S(2)}, u32[]{:S(2)}) collective-permute-start(f32[72,384]{1,0:T(8,128)S(1)} %get-tuple-element.91), channel_id=1, source_target_pairs={{0,1},{2,3},{1,0},{3,2},{4,5},{6,7},{5,4},{7,6},{8,9},{10,11},{9,8... | collective-permute-start | bytes 331784 | tf_op jit(solution)/shard_map/ppermute | solution.py:699
  67.9 11.5 %collective-permute-start.16 = (f32[8,128]{1,0:T(8,128)S(1)}, f32[8,128]{1,0:T(8,128)S(1)}, u32[]{:S(2)}, u32[]{:S(2)}) collective-permute-start(f32[8,128]{1,0:T(8,128)S(1)} %get-tuple-element.90), channel_id=1, source_target_pairs={{4,3},{8,7},{12,11},{16,15},{20,19},{24,23},{28,27},{32,31},{36,35... | collective-permute-start | bytes 12296 | tf_op jit(solution)/shard_map/ppermute | solution.py:698

commit v3 on v2

--- a/solution.py
+++ b/solution.py
@@ -19,6 +19,7 @@
 VELOCITY_Z = ([(2, 2), (2, 1), (0, 1), (1, 1)], [(2, 0), (0, 0), (0, 1), (1, 0), (1, 1)])
 
 BULK = 2 * 10**6
+EARLY = 8
 CB, LAME, MU2, DECAY, DAMP, ISO, SCALE = range(7)
 
 
@@ -543,24 +544,31 @@
 
 def velocity_bulk(stress, props, velocity, peak):
     def kernel(sf, sc, pf, pc, vf, vc, *rest):
-        kf, kc, of, oc, okf, okc = rest
+        kf, of, oc, okf = rest
         velocity_rows(Grid(sf, 1.0), vf, of, pf)
         velocity_rows(Grid(sc, 3.0), vc, oc, pc)
-        peak_rows(sf, pf, kf, okf)
-        peak_rows(sc, pc, kc, okc)
-
-    outs = [like(x) for x in (*velocity, *peak)]
-    out = call(kernel, "velocity_bulk", (), (*stress, *props, *velocity, *peak), outs, [], BULK)
-    return out[:2], out[2:]
-
-
-def stress_bulk(velocity, props, stress, memory):
-    def kernel(vf, vc, pf, pc, sf, sc, mf, mc, osf, osc, omf, omc):
+        peak_rows(sf, pf, kf, okf, 0, EARLY)
+
+    outs = [like(x) for x in (*velocity, peak[0])]
+    out = call(kernel, "velocity_bulk", (), (*stress, *props, *velocity, peak[0]), outs, [], BULK)
+    return out[:2], out[2]
+
+
+def stress_bulk(velocity, props, stress, memory, peak=(), early=None):
+    def kernel(vf, vc, pf, pc, sf, sc, mf, mc, *rest):
+        osf, osc, omf, omc = rest[len(rest) - 6 : -2] if peak else rest
         stress_rows(Grid(vf, 1.0), sf, mf, osf, omf, pf)
         stress_rows(Grid(vc, 3.0), sc, mc, osc, omc, pc)
-
-    outs = [like(x) for x in (*stress, *memory)]
-    return call(kernel, "stress_bulk", (), (*velocity, *props, *stress, *memory), outs, [], BULK)
+        if peak:
+            (kf, kc, ef), (okf, okc) = rest[:3], rest[-2:]
+            okf[0:EARLY] = ef[0:EARLY]
+            peak_rows(sf, pf, kf, okf, EARLY, sf.shape[1])
+            peak_rows(sc, pc, kc, okc)
+
+    outs = [like(x) for x in (*stress, *memory, *peak)]
+    more = (*peak, early) if peak else ()
+    out = call(kernel, "stress_bulk", (), (*velocity, *props, *stress, *memory, *more), outs, [], BULK)
+    return out[:2], out[2:4], tuple(out[4:])
 
 
 def velocity_finish(sizes, interp, restrict, halos, props, velocity):
@@ -673,7 +681,7 @@
     return jnp.maximum(jnp.maximum(a, b), c)
 
 
-def peak_rows(stress, props, peak, out, width=2):
+def peak_rows(stress, props, peak, out, first=0, end=None, width=2):
     def step(i, carry):
         x = pl.ds(i * width, width)
         xx, yy, zz, xy, xz, yz = [stress[comp, x] for comp in range(6)]
@@ -682,7 +690,7 @@
         out[x] = jnp.maximum(peak[x], principal)
         return carry
 
-    lax.fori_loop(0, stress.shape[1] // width, step, 0)
+    lax.fori_loop(first // width, (end or stress.shape[1]) // width, step, 0)
 
 
 def exchanged(arrays):
@@ -728,19 +736,22 @@
         if step == 0:
             velocity, props = first_bulk(zone_table, (zone_fine, zone_coarse), stress, velocity)
         else:
-            velocity, peak = velocity_bulk(stress, props, velocity, peak)
+            velocity, early = velocity_bulk(stress, props, velocity, peak)
         velocity, outgoing = velocity_finish(
             sizes, interp_weight, restrict_weight, halos, props, velocity
         )
         halos = exchanged(outgoing)
-        bulk = stress_bulk(velocity, props, stress, memory)
+        if step == 0:
+            stress, memory, _ = stress_bulk(velocity, props, stress, memory)
+        else:
+            stress, memory, peak = stress_bulk(velocity, props, stress, memory, peak, early)
         if step + 1 < STEPS:
             stress, memory, outgoing = stress_finish(
-                sizes, interp_weight, restrict_weight, halos, props, bulk[:2], bulk[2:]
+                sizes, interp_weight, restrict_weight, halos, props, stress, memory
             )
         else:
             velocity, stress, memory, peak = last_finish(
-                sizes, interp_weight, halos, props, bulk[:2], bulk[2:], peak, velocity
+                sizes, interp_weight, halos, props, stress, memory, peak, velocity
             )
     return (velocity[0], stress[0], memory[0], peak[0], velocity[1], stress[1], memory[1], peak[1])
 

time: 85.4 us -> 85.7 us (level)
    ppermute x4, starting transfers between devices: 14.2 us -> 15.8 us  [exchanged(): depO = lax.ppermute(depO, 'depth', swaps(depth, 1))]
    ppermute x4, starting transfers between devices: 29.8 us -> 28.4 us  [exchanged(): diag = lax.ppermute(diag, ('lat', 'depth'), across)]
where the time goes in v3:
time: 85.7 us; the launch traced here: 85.4 us
  starting transfers between devices  53.9 us (63%)
  Pallas kernels  26.4 us (31%)
  local copies, waits for them, and re-layouts  3.85 us (4%)
  between operations  1.21 us (1%)
    ppermute x4, starting transfers between devices, exchanged(): diag = lax.ppermute(diag, ('lat', 'depth'), across)  28.4 us
    pallas_call x9, Pallas kernels, call(): pl.pallas_call(kernel, name=name, out_shape=outs, in_specs=[SMEM] * len(s...  26.4 us
    ppermute x4, starting transfers between devices, exchanged(): depO = lax.ppermute(depO, 'depth', swaps(depth, 1))  15.8 us
    ppermute x4, starting transfers between devices, exchanged(): latE = lax.ppermute(latE, 'lat', swaps(lat, 0))  6.47 us
    unnamed x26, local copies, waits for them, and re-layouts  3.85 us
    ppermute x4, starting transfers between devices, exchanged(): latO = lax.ppermute(latO, 'lat', swaps(lat, 1))  2.4 us
  transfers between devices with their start and end apart: 20, of which 0 were waited for; matrix products, arithmetic and copies ran while one was open for 0% of the time, Pallas kernels for 17%

profile of v3, /device:TPU:4, one launch (start us, length us, event | category | flops | bytes accessed | tf_op | source)
XLA Modules:
  0.0 85.4 jit_solution(7828344124226902595)
XLA Ops:
  0.7 3.1 %pack_stress.1 = (f32[72,384]{1,0:T(8,128)}, f32[8,128]{1,0:T(8,128)}, f32[72,384]{1,0:T(8,128)}, f32[144,384]{1,0:T(8,128)}, f32[144,384]{1,0:T(8,128)}) custom-call(s32[2,3]{1,0:T(2,128)} %restrict.7, f32[6,12,16,384]{3,2,1,0:T(8,128)} %sf.1, f32[6,4,32,128]{3,2,1,0:T(8,128)} %sc.1), custom_call_target="tpu_custom_call" | custom-call | flops 1000000 | bytes 2830336 | tf_op jit(solution)/shard_map/pack_stress/pallas_call | solution.py:454
  3.7 0.6 collective-permute-start.3
  4.4 2.2 %collective-permute-start.4 = (f32[144,384]{1,0:T(8,128)}, f32[144,384]{1,0:T(8,128)S(1)}, u32[]{:S(2)}, u32[]{:S(2)}) collective-permute-start(f32[144,384]{1,0:T(8,128)} %get-tuple-element.65), channel_id=1, source_target_pairs={{0,4},{8,12},{16,20},{24,28},{32,36},{40,44},{48,52},{56,60},{64,6... | collective-permute-start | bytes 663560 | tf_op jit(solution)/shard_map/ppermute | solution.py:709
  6.5 6.5 %collective-permute-start = (f32[72,384]{1,0:T(8,128)}, f32[72,384]{1,0:T(8,128)S(1)}, u32[]{:S(2)}, u32[]{:S(2)}) collective-permute-start(f32[72,384]{1,0:T(8,128)} %get-tuple-element.61), channel_id=1, source_target_pairs={{1,2},{3,0},{2,1},{0,3},{5,6},{7,4},{6,5},{4,7},{9,10},{11,8},{10,... | collective-permute-start | bytes 331784 | tf_op jit(solution)/shard_map/ppermute | solution.py:705
  13.0 0.8 collective-permute-start.2
  13.8 7.3 %collective-permute-start.1 = (f32[8,128]{1,0:T(8,128)}, f32[8,128]{1,0:T(8,128)S(1)}, u32[]{:S(2)}, u32[]{:S(2)}) collective-permute-start(f32[8,128]{1,0:T(8,128)} %get-tuple-element.62), channel_id=1, source_target_pairs={{4,3},{8,7},{12,11},{16,15},{20,19},{24,23},{28,27},{32,31},{36,35... | collective-permute-start | bytes 12296 | tf_op jit(solution)/shard_map/ppermute | solution.py:706
  21.2 0.0 copy-start.1
  21.2 1.0 %copy-done.1 = f32[6,4,32,128]{3,2,1,0:T(8,128)S(1)} copy-done((f32[6,4,32,128]{3,2,1,0:T(8,128)S(1)}, f32[6,4,32,128]{3,2,1,0:T(8,128)}, u32[]{:S(2)}) %copy-start.1) | copy-done | bytes 393240
  22.2 1.2 %copy-done.4 = f32[3,12,16,384]{3,2,1,0:T(8,128)S(1)} copy-done((f32[3,12,16,384]{3,2,1,0:T(8,128)S(1)}, f32[3,12,16,384]{3,2,1,0:T(8,128)}, u32[]{:S(2)}) %copy-start.4) | copy-done | bytes 884760
  23.4 1.0 %copy-done.6 = s32[12,16,384]{2,1,0:T(8,128)S(1)} copy-done((s32[12,16,384]{2,1,0:T(8,128)S(1)}, s32[12,16,384]{2,1,0:T(8,128)}, u32[]{:S(2)}) %copy-start.6) | copy-done | bytes 294936
  24.3 0.7 copy-done.12
  25.0 4.5 %first_bulk.1 = (f32[3,12,16,384]{3,2,1,0:T(8,128)S(1)}, f32[3,4,32,128]{3,2,1,0:T(8,128)S(1)}, f32[7,12,16,384]{3,2,1,0:T(8,128)S(1)}, f32[7,4,32,128]{3,2,1,0:T(8,128)S(1)}) custom-call(f32[8,5]{1,0:T(8,128)S(1)} %copy-done.12, s32[12,16,384]{2,1,0:T(8,128)S(1)} %copy-done.6, s32[4,32,128]{2,1,0:T(8,128)S(1)} %copy-done.8, f32[6,12,16,384]{3,2,1,0:T(8,128)S(1)} %copy-done, ...), custom_call_target="tpu_custom_call" | custom-call | flops 2000000 | bytes 7208960 | tf_op jit(solution)/shard_map/first_bulk/pallas_call | solution.py:454
  29.5 0.0 collective-permute-done.rest_0_
  29.5 0.0 collective-permute-done.2.rest_2_
  29.5 0.0 collective-permute-done.4.rest_4_
  29.6 0.0 copy-start.2
  29.6 0.0 copy-start.5
  29.6 1.1 %velocity_finish.2 = (f32[3,12,16,384]{3,2,1,0:T(8,128)S(1)}, f32[3,4,32,128]{3,2,1,0:T(8,128)S(1)}, f32[72,384]{1,0:T(8,128)S(1)}, f32[8,128]{1,0:T(8,128)S(1)}...) custom-call(s32[2,3]{1,0:T(2,128)S(1)} %copy-done.11, s32[2,3]{1,0:T(2,128)S(1)} %copy-done.10, ...), custom_call_target="tpu_custom_call" | custom-call | flops 10000000 | bytes 6021120 | tf_op jit(solution)/shard_map/velocity_finish/pallas_call | solution.py:454
  30.7 0.1 collective-permute-start.8
  30.8 0.1 collective-permute-start.9
  30.9 0.6 collective-permute-start.5
  31.5 8.8 %collective-permute-start.6 = (f32[8,128]{1,0:T(8,128)S(1)}, f32[8,128]{1,0:T(8,128)S(1)}, u32[]{:S(2)}, u32[]{:S(2)}) collective-permute-start(f32[8,128]{1,0:T(8,128)S(1)} %get-tuple-element.71), channel_id=1, source_target_pairs={{4,3},{8,7},{12,11},{16,15},{20,19},{24,23},{28,27},{32,31},{36,35... | collective-permute-start | bytes 12296 | tf_op jit(solution)/shard_map/ppermute | solution.py:706
  40.3 2.2 %stress_bulk.2 = (f32[6,12,16,384]{3,2,1,0:T(8,128)S(1)}, f32[6,4,32,128]{3,2,1,0:T(8,128)S(1)}, f32[6,12,16,384]{3,2,1,0:T(8,128)S(1)}, f32[6,4,32,128]{3,2,1,0:T(8,128)S(1)}) custom-call(f32[3,12,16,384]{3,2,1,0:T(8,128)S(1)} %get-tuple-element.75.vf, f32[3,4,32,128]{3,2,1,0:T(8,128)S(1)} %get-tuple-element.76.vc, ...), custom_call_target="tpu_custom_call" | custom-call | flops 2000000 | bytes 12255232 | tf_op jit(solution)/shard_map/stress_bulk/pallas_call | solution.py:454
  42.6 0.0 collective-permute-done.6.rest_1_
  42.6 0.0 collective-permute-done.5.rest_0_
  42.6 0.0 collective-permute-done.8.rest_3_
  42.6 0.0 collective-permute-done.9.rest_4_
  42.6 0.0 copy-start.3
  42.6 1.4 %stress_finish.1 = (f32[6,12,16,384]{3,2,1,0:T(8,128)S(1)}, f32[6,4,32,128]{3,2,1,0:T(8,128)S(1)}, f32[6,12,16,384]{3,2,1,0:T(8,128)S(1)}, f32[6,4,32,128]{3,2,1...) custom-call(s32[2,3]{1,0:T(2,128)S(1)} %copy-done.11, ...), custom_call_target="tpu_custom_call" | custom-call | flops 20000000 | bytes 12509184 | tf_op jit(solution)/shard_map/stress_finish/pallas_call | solution.py:454
  44.0 1.6 %collective-permute-start.13 = (f32[144,384]{1,0:T(8,128)S(1)}, f32[144,384]{1,0:T(8,128)S(1)}, u32[]{:S(2)}, u32[]{:S(2)}) collective-permute-start(f32[144,384]{1,0:T(8,128)S(1)} %get-tuple-element.84), channel_id=1, source_target_pairs={{4,8},{12,16},{20,24},{28,32},{36,40},{44,48},{52,56},{60,64},{68,... | collective-permute-start | bytes 663560 | tf_op jit(solution)/shard_map/ppermute | solution.py:708
  45.6 2.2 %collective-permute-start.14 = (f32[144,384]{1,0:T(8,128)S(1)}, f32[144,384]{1,0:T(8,128)S(1)}, u32[]{:S(2)}, u32[]{:S(2)}) collective-permute-start(f32[144,384]{1,0:T(8,128)S(1)} %get-tuple-element.85), channel_id=1, source_target_pairs={{0,4},{8,12},{16,20},{24,28},{32,36},{40,44},{48,52},{56,60},{64,6... | collective-permute-start | bytes 663560 | tf_op jit(solution)/shard_map/ppermute | solution.py:709
  47.8 4.8 %collective-permute-start.10 = (f32[72,384]{1,0:T(8,128)S(1)}, f32[72,384]{1,0:T(8,128)S(1)}, u32[]{:S(2)}, u32[]{:S(2)}) collective-permute-start(f32[72,384]{1,0:T(8,128)S(1)} %get-tuple-element.81), channel_id=1, source_target_pairs={{1,2},{3,0},{2,1},{0,3},{5,6},{7,4},{6,5},{4,7},{9,10},{11,8},{10,... | collective-permute-start | bytes 331784 | tf_op jit(solution)/shard_map/ppermute | solution.py:705
  52.7 0.0 collective-permute-start.12
  52.7 4.4 %collective-permute-start.11 = (f32[8,128]{1,0:T(8,128)S(1)}, f32[8,128]{1,0:T(8,128)S(1)}, u32[]{:S(2)}, u32[]{:S(2)}) collective-permute-start(f32[8,128]{1,0:T(8,128)S(1)} %get-tuple-element.82), channel_id=1, source_target_pairs={{4,3},{8,7},{12,11},{16,15},{20,19},{24,23},{28,27},{32,31},{36,35... | collective-permute-start | bytes 12296 | tf_op jit(solution)/shard_map/ppermute | solution.py:706
  57.1 3.7 %velocity_bulk.1 = (f32[3,12,16,384]{3,2,1,0:T(8,128)S(1)}, f32[3,4,32,128]{3,2,1,0:T(8,128)S(1)}, f32[12,16,384]{2,1,0:T(8,128)S(1)}) custom-call(f32[6,12,16,384]{3,2,1,0:T(8,128)S(1)} %get-tuple-element.86.sf, f32[6,4,32,128]{3,2,1,0:T(8,128)S(1)} %get-tuple-element.87.sc, f32[7,12,16,384]{3,2,1,0:T(8,128)S(1)} %get-tuple-element.66.rest_5_.pf, ...), custom_call_target="tpu_custom_call" | custom-call | flops 2000000 | bytes 7438336 | tf_op jit(solution)/shard_map/velocity_bulk/pallas_call | solution.py:454
  60.8 0.0 collective-permute-done.10.rest_0_
  60.8 0.0 collective-permute-done.12.rest_2_
  60.8 0.0 copy-start.9
  60.9 1.1 %velocity_finish.3 = (f32[3,12,16,384]{3,2,1,0:T(8,128)S(1)}, f32[3,4,32,128]{3,2,1,0:T(8,128)S(1)}, f32[72,384]{1,0:T(8,128)S(1)}, f32[8,128]{1,0:T(8,128)S(1)}...) custom-call(s32[2,3]{1,0:T(2,128)S(1)} %copy-done.11, s32[2,3]{1,0:T(2,128)S(1)} %copy-done.10, ...), custom_call_target="tpu_custom_call" | custom-call | flops 10000000 | bytes 6021120 | tf_op jit(solution)/shard_map/velocity_finish/pallas_call | solution.py:454
  62.0 0.1 collective-permute-start.18
  62.1 2.0 %collective-permute-start.19 = (f32[144,384]{1,0:T(8,128)S(1)}, f32[144,384]{1,0:T(8,128)S(1)}, u32[]{:S(2)}, u32[]{:S(2)}) collective-permute-start(f32[144,384]{1,0:T(8,128)S(1)} %get-tuple-element.94), channel_id=1, source_target_pairs={{0,4},{8,12},{16,20},{24,28},{32,36},{40,44},{48,52},{56,60},{64,6... | collective-permute-start | bytes 663560 | tf_op jit(solution)/shard_map/ppermute | solution.py:709
  64.1 3.8 %collective-permute-start.15 = (f32[72,384]{1,0:T(8,128)S(1)}, f32[72,384]{1,0:T(8,128)S(1)}, u32[]{:S(2)}, u32[]{:S(2)}) collective-permute-start(f32[72,384]{1,0:T(8,128)S(1)} %get-tuple-element.90), channel_id=1, source_target_pairs={{1,2},{3,0},{2,1},{0,3},{5,6},{7,4},{6,5},{4,7},{9,10},{11,8},{10,... | collective-permute-start | bytes 331784 | tf_op jit(solution)/shard_map/ppermute | solution.py:705
  67.9 0.0 collective-permute-start.17
  67.9 7.8 %collective-permute-start.16 = (f32[8,128]{1,0:T(8,128)S(1)}, f32[8,128]{1,0:T(8,128)S(1)}, u32[]{:S(2)}, u32[]{:S(2)}) collective-permute-start(f32[8,128]{1,0:T(8,128)S(1)} %get-tuple-element.91), channel_id=1, source_target_pairs={{4,3},{8,7},{12,11},{16,15},{20,19},{24,23},{28,27},{32,31},{36,35... | collective-permute-start | bytes 12296 | tf_op jit(solution)/shard_map/ppermute | solution.py:706
  75.8 3.9 %stress_bulk.3 = (f32[6,12,16,384]{3,2,1,0:T(8,128)S(1)}, f32[6,4,32,128]{3,2,1,0:T(8,128)S(1)}, f32[6,12,16,384]{3,2,1,0:T(8,128)S(1)}, f32[6,4,32,128]{3,2,1,0...) custom-call(f32[3,12,16,384]{3,2,1,0:T(8,128)S(1)} %get-tuple-element.95.vf.rest_13_, ...), custom_call_target="tpu_custom_call" | custom-call | flops 2000000 | bytes 13271040 | tf_op jit(solution)/shard_map/stress_bulk/pallas_call | solution.py:454
  79.7 0.0 collective-permute-done.15.rest_0_
  79.7 0.0 collective-permute-done.17.rest_2_
  79.7 5.5 %last_finish.1 = (f32[3,12,16,384]{3,2,1,0:T(8,128)}, f32[3,4,32,128]{3,2,1,0:T(8,128)}, f32[6,12,16,384]{3,2,1,0:T(8,128)}, f32[6,4,32,128]{3,2,1,0:T(8,128)}, ...) custom-call(s32[2,3]{1,0:T(2,128)S(1)} %copy-done.11, ...), custom_call_target="tpu_custom_call" | custom-call | flops 20000000 | bytes 14725120 | tf_op jit(solution)/shard_map/last_finish/pallas_call | solution.py:454
  (27 shorter events, 0.1 us)
Async XLA Ops:
  0.6 20.5 %copy-start = (f32[6,12,16,384]{3,2,1,0:T(8,128)S(1)}, f32[6,12,16,384]{3,2,1,0:T(8,128)}, u32[]{:S(2)}) copy-start(f32[6,12,16,384]{3,2,1,0:T(8,128)} %sf.1) | copy-start | bytes 5308420
  0.6 20.5 %copy-start.8 = (s32[4,32,128]{2,1,0:T(8,128)S(1)}, s32[4,32,128]{2,1,0:T(8,128)}, u32[]{:S(2)}) copy-start(s32[4,32,128]{2,1,0:T(8,128)} %rest_1_.2) | copy-start | bytes 196612
  0.7 20.5 %copy-start.7 = (f32[3,4,32,128]{3,2,1,0:T(8,128)S(1)}, f32[3,4,32,128]{3,2,1,0:T(8,128)}, u32[]{:S(2)}) copy-start(f32[3,4,32,128]{3,2,1,0:T(8,128)} %rest_5_.1) | copy-start | bytes 589828
  3.7 25.8 %collective-permute-start.3 = (f32[144,384]{1,0:T(8,128)}, f32[144,384]{1,0:T(8,128)S(1)}, u32[]{:S(2)}, u32[]{:S(2)}) collective-permute-start(f32[144,384]{1,0:T(8,128)} %get-tuple-element.64), channel_id=1, source_target_pairs={{4,8},{12,16},{20,24},{28,32},{36,40},{44,48},{52,56},{60,64},{68,... | collective-permute-start | bytes 663560 | tf_op jit(solution)/shard_map/ppermute | solution.py:708
  4.4 25.2 %collective-permute-start.4 = (f32[144,384]{1,0:T(8,128)}, f32[144,384]{1,0:T(8,128)S(1)}, u32[]{:S(2)}, u32[]{:S(2)}) collective-permute-start(f32[144,384]{1,0:T(8,128)} %get-tuple-element.65), channel_id=1, source_target_pairs={{0,4},{8,12},{16,20},{24,28},{32,36},{40,44},{48,52},{56,60},{64,6... | collective-permute-start | bytes 663560 | tf_op jit(solution)/shard_map/ppermute | solution.py:709
  6.5 23.0 %collective-permute-start = (f32[72,384]{1,0:T(8,128)}, f32[72,384]{1,0:T(8,128)S(1)}, u32[]{:S(2)}, u32[]{:S(2)}) collective-permute-start(f32[72,384]{1,0:T(8,128)} %get-tuple-element.61), channel_id=1, source_target_pairs={{1,2},{3,0},{2,1},{0,3},{5,6},{7,4},{6,5},{4,7},{9,10},{11,8},{10,... | collective-permute-start | bytes 331784 | tf_op jit(solution)/shard_map/ppermute | solution.py:705
  13.0 16.5 %collective-permute-start.2 = (f32[72,384]{1,0:T(8,128)}, f32[72,384]{1,0:T(8,128)S(1)}, u32[]{:S(2)}, u32[]{:S(2)}) collective-permute-start(f32[72,384]{1,0:T(8,128)} %get-tuple-element.63), channel_id=1, source_target_pairs={{0,1},{2,3},{1,0},{3,2},{4,5},{6,7},{5,4},{7,6},{8,9},{10,11},{9,8... | collective-permute-start | bytes 331784 | tf_op jit(solution)/shard_map/ppermute | solution.py:707
  13.8 15.7 %collective-permute-start.1 = (f32[8,128]{1,0:T(8,128)}, f32[8,128]{1,0:T(8,128)S(1)}, u32[]{:S(2)}, u32[]{:S(2)}) collective-permute-start(f32[8,128]{1,0:T(8,128)} %get-tuple-element.62), channel_id=1, source_target_pairs={{4,3},{8,7},{12,11},{16,15},{20,19},{24,23},{28,27},{32,31},{36,35... | collective-permute-start | bytes 12296 | tf_op jit(solution)/shard_map/ppermute | solution.py:706
  21.2 1.0 %copy-start.1 = (f32[6,4,32,128]{3,2,1,0:T(8,128)S(1)}, f32[6,4,32,128]{3,2,1,0:T(8,128)}, u32[]{:S(2)}) copy-start(f32[6,4,32,128]{3,2,1,0:T(8,128)} %sc.1) | copy-start | bytes 1179652
  22.2 1.2 %copy-start.4 = (f32[3,12,16,384]{3,2,1,0:T(8,128)S(1)}, f32[3,12,16,384]{3,2,1,0:T(8,128)}, u32[]{:S(2)}) copy-start(f32[3,12,16,384]{3,2,1,0:T(8,128)} %rest_4_.1) | copy-start | bytes 2654212
  23.4 1.0 %copy-start.6 = (s32[12,16,384]{2,1,0:T(8,128)S(1)}, s32[12,16,384]{2,1,0:T(8,128)}, u32[]{:S(2)}) copy-start(s32[12,16,384]{2,1,0:T(8,128)} %rest_0_.3) | copy-start | bytes 884740
  24.3 0.7 copy-start.12
  25.0 4.5 %copy-start.10 = (s32[2,3]{1,0:T(2,128)S(1)}, s32[2,3]{1,0:T(2,128)}, u32[]{:S(2)}) copy-start(s32[2,3]{1,0:T(2,128)} %restrict.7) | copy-start | bytes 76
  25.0 4.6 %copy-start.11 = (s32[2,3]{1,0:T(2,128)S(1)}, s32[2,3]{1,0:T(2,128)}, u32[]{:S(2)}) copy-start(s32[2,3]{1,0:T(2,128)} %interp.7) | copy-start | bytes 76
  29.6 10.8 %copy-start.2 = (f32[6,12,16,384]{3,2,1,0:T(8,128)S(1)}, f32[6,12,16,384]{3,2,1,0:T(8,128)}, u32[]{:S(2)}) copy-start(f32[6,12,16,384]{3,2,1,0:T(8,128)} %mf.1) | copy-start | bytes 5308420
  29.6 10.8 %copy-start.5 = (f32[6,4,32,128]{3,2,1,0:T(8,128)S(1)}, f32[6,4,32,128]{3,2,1,0:T(8,128)}, u32[]{:S(2)}) copy-start(f32[6,4,32,128]{3,2,1,0:T(8,128)} %mc.1) | copy-start | bytes 1179652
  30.7 11.9 %collective-permute-start.8 = (f32[144,384]{1,0:T(8,128)S(1)}, f32[144,384]{1,0:T(8,128)S(1)}, u32[]{:S(2)}, u32[]{:S(2)}) collective-permute-start(f32[144,384]{1,0:T(8,128)S(1)} %get-tuple-element.73), channel_id=1, source_target_pairs={{4,8},{12,16},{20,24},{28,32},{36,40},{44,48},{52,56},{60,64},{68,... | collective-permute-start | bytes 663560 | tf_op jit(solution)/shard_map/ppermute | solution.py:708
  30.8 11.8 %collective-permute-start.9 = (f32[144,384]{1,0:T(8,128)S(1)}, f32[144,384]{1,0:T(8,128)S(1)}, u32[]{:S(2)}, u32[]{:S(2)}) collective-permute-start(f32[144,384]{1,0:T(8,128)S(1)} %get-tuple-element.74), channel_id=1, source_target_pairs={{0,4},{8,12},{16,20},{24,28},{32,36},{40,44},{48,52},{56,60},{64,6... | collective-permute-start | bytes 663560 | tf_op jit(solution)/shard_map/ppermute | solution.py:709
  30.9 11.7 %collective-permute-start.5 = (f32[72,384]{1,0:T(8,128)S(1)}, f32[72,384]{1,0:T(8,128)S(1)}, u32[]{:S(2)}, u32[]{:S(2)}) collective-permute-start(f32[72,384]{1,0:T(8,128)S(1)} %get-tuple-element.70), channel_id=1, source_target_pairs={{1,2},{3,0},{2,1},{0,3},{5,6},{7,4},{6,5},{4,7},{9,10},{11,8},{10,... | collective-permute-start | bytes 331784 | tf_op jit(solution)/shard_map/ppermute | solution.py:705
  31.5 11.1 %collective-permute-start.7 = (f32[72,384]{1,0:T(8,128)S(1)}, f32[72,384]{1,0:T(8,128)S(1)}, u32[]{:S(2)}, u32[]{:S(2)}) collective-permute-start(f32[72,384]{1,0:T(8,128)S(1)} %get-tuple-element.72), channel_id=1, source_target_pairs={{0,1},{2,3},{1,0},{3,2},{4,5},{6,7},{5,4},{7,6},{8,9},{10,11},{9,8... | collective-permute-start | bytes 331784 | tf_op jit(solution)/shard_map/ppermute | solution.py:707
  31.5 11.0 %collective-permute-start.6 = (f32[8,128]{1,0:T(8,128)S(1)}, f32[8,128]{1,0:T(8,128)S(1)}, u32[]{:S(2)}, u32[]{:S(2)}) collective-permute-start(f32[8,128]{1,0:T(8,128)S(1)} %get-tuple-element.71), channel_id=1, source_target_pairs={{4,3},{8,7},{12,11},{16,15},{20,19},{24,23},{28,27},{32,31},{36,35... | collective-permute-start | bytes 12296 | tf_op jit(solution)/shard_map/ppermute | solution.py:706
  42.6 14.5 %copy-start.3 = (f32[12,16,384]{2,1,0:T(8,128)S(1)}, f32[12,16,384]{2,1,0:T(8,128)}, u32[]{:S(2)}) copy-start(f32[12,16,384]{2,1,0:T(8,128)} %rest_0_.5) | copy-start | bytes 884740
  44.0 16.8 %collective-permute-start.13 = (f32[144,384]{1,0:T(8,128)S(1)}, f32[144,384]{1,0:T(8,128)S(1)}, u32[]{:S(2)}, u32[]{:S(2)}) collective-permute-start(f32[144,384]{1,0:T(8,128)S(1)} %get-tuple-element.84), channel_id=1, source_target_pairs={{4,8},{12,16},{20,24},{28,32},{36,40},{44,48},{52,56},{60,64},{68,... | collective-permute-start | bytes 663560 | tf_op jit(solution)/shard_map/ppermute | solution.py:708
  45.6 15.2 %collective-permute-start.14 = (f32[144,384]{1,0:T(8,128)S(1)}, f32[144,384]{1,0:T(8,128)S(1)}, u32[]{:S(2)}, u32[]{:S(2)}) collective-permute-start(f32[144,384]{1,0:T(8,128)S(1)} %get-tuple-element.85), channel_id=1, source_target_pairs={{0,4},{8,12},{16,20},{24,28},{32,36},{40,44},{48,52},{56,60},{64,6... | collective-permute-start | bytes 663560 | tf_op jit(solution)/shard_map/ppermute | solution.py:709
  47.8 13.0 %collective-permute-start.10 = (f32[72,384]{1,0:T(8,128)S(1)}, f32[72,384]{1,0:T(8,128)S(1)}, u32[]{:S(2)}, u32[]{:S(2)}) collective-permute-start(f32[72,384]{1,0:T(8,128)S(1)} %get-tuple-element.81), channel_id=1, source_target_pairs={{1,2},{3,0},{2,1},{0,3},{5,6},{7,4},{6,5},{4,7},{9,10},{11,8},{10,... | collective-permute-start | bytes 331784 | tf_op jit(solution)/shard_map/ppermute | solution.py:705
  52.7 8.1 %collective-permute-start.12 = (f32[72,384]{1,0:T(8,128)S(1)}, f32[72,384]{1,0:T(8,128)S(1)}, u32[]{:S(2)}, u32[]{:S(2)}) collective-permute-start(f32[72,384]{1,0:T(8,128)S(1)} %get-tuple-element.83), channel_id=1, source_target_pairs={{0,1},{2,3},{1,0},{3,2},{4,5},{6,7},{5,4},{7,6},{8,9},{10,11},{9,8... | collective-permute-start | bytes 331784 | tf_op jit(solution)/shard_map/ppermute | solution.py:707
  52.7 8.1 %collective-permute-start.11 = (f32[8,128]{1,0:T(8,128)S(1)}, f32[8,128]{1,0:T(8,128)S(1)}, u32[]{:S(2)}, u32[]{:S(2)}) collective-permute-start(f32[8,128]{1,0:T(8,128)S(1)} %get-tuple-element.82), channel_id=1, source_target_pairs={{4,3},{8,7},{12,11},{16,15},{20,19},{24,23},{28,27},{32,31},{36,35... | collective-permute-start | bytes 12296 | tf_op jit(solution)/shard_map/ppermute | solution.py:706
  60.8 14.9 %copy-start.9 = (f32[4,32,128]{2,1,0:T(8,128)S(1)}, f32[4,32,128]{2,1,0:T(8,128)}, u32[]{:S(2)}) copy-start(f32[4,32,128]{2,1,0:T(8,128)} %rest_1_.3) | copy-start | bytes 196612
  62.0 17.7 %collective-permute-start.18 = (f32[144,384]{1,0:T(8,128)S(1)}, f32[144,384]{1,0:T(8,128)S(1)}, u32[]{:S(2)}, u32[]{:S(2)}) collective-permute-start(f32[144,384]{1,0:T(8,128)S(1)} %get-tuple-element.93), channel_id=1, source_target_pairs={{4,8},{12,16},{20,24},{28,32},{36,40},{44,48},{52,56},{60,64},{68,... | collective-permute-start | bytes 663560 | tf_op jit(solution)/shard_map/ppermute | solution.py:708
  62.1 17.6 %collective-permute-start.19 = (f32[144,384]{1,0:T(8,128)S(1)}, f32[144,384]{1,0:T(8,128)S(1)}, u32[]{:S(2)}, u32[]{:S(2)}) collective-permute-start(f32[144,384]{1,0:T(8,128)S(1)} %get-tuple-element.94), channel_id=1, source_target_pairs={{0,4},{8,12},{16,20},{24,28},{32,36},{40,44},{48,52},{56,60},{64,6... | collective-permute-start | bytes 663560 | tf_op jit(solution)/shard_map/ppermute | solution.py:709
  64.1 15.6 %collective-permute-start.15 = (f32[72,384]{1,0:T(8,128)S(1)}, f32[72,384]{1,0:T(8,128)S(1)}, u32[]{:S(2)}, u32[]{:S(2)}) collective-permute-start(f32[72,384]{1,0:T(8,128)S(1)} %get-tuple-element.90), channel_id=1, source_target_pairs={{1,2},{3,0},{2,1},{0,3},{5,6},{7,4},{6,5},{4,7},{9,10},{11,8},{10,... | collective-permute-start | bytes 331784 | tf_op jit(solution)/shard_map/ppermute | solution.py:705
  67.9 11.8 %collective-permute-start.17 = (f32[72,384]{1,0:T(8,128)S(1)}, f32[72,384]{1,0:T(8,128)S(1)}, u32[]{:S(2)}, u32[]{:S(2)}) collective-permute-start(f32[72,384]{1,0:T(8,128)S(1)} %get-tuple-element.92), channel_id=1, source_target_pairs={{0,1},{2,3},{1,0},{3,2},{4,5},{6,7},{5,4},{7,6},{8,9},{10,11},{9,8... | collective-permute-start | bytes 331784 | tf_op jit(solution)/shard_map/ppermute | solution.py:707
  67.9 11.7 %collective-permute-start.16 = (f32[8,128]{1,0:T(8,128)S(1)}, f32[8,128]{1,0:T(8,128)S(1)}, u32[]{:S(2)}, u32[]{:S(2)}) collective-permute-start(f32[8,128]{1,0:T(8,128)S(1)} %get-tuple-element.91), channel_id=1, source_target_pairs={{4,3},{8,7},{12,11},{16,15},{20,19},{24,23},{28,27},{32,31},{36,35... | collective-permute-start | bytes 12296 | tf_op jit(solution)/shard_map/ppermute | solution.py:706
